TPU v7x, 256 devices: a whole 4x4x8 slice. The times are simulated.
256 devices in a mesh: group: 2 (over x_lo), batch: 128 (over x_hi, z, y, core).
Axes of the slice: x: 4 (x_hi: 2, x_lo: 2; x = x_hi * 2 + x_lo), y: 4, z: 8, core: 2. Of those that a mesh axis runs over, the one named last changes fastest.
Arguments:
- teacher_image: bfloat16 [8192, 768], P('batch'), may hold values from -16 to 16
- teacher_text: bfloat16 [8192, 768], P('batch'), may hold values from -16 to 16
- student_image: bfloat16 [8192, 768], P('batch'), may hold values from -16 to 16
- student_text: bfloat16 [8192, 768], P('batch'), may hold values from -16 to 16
- scales: float32 [2], replicated, may hold values from 0.2 to 0.3
Outputs:
- embedding_grads: float32 [2, 8192, 768], P('group', 'batch')
All inputs are finite; a program needn't handle non-finite values.
Results may differ from a plain program's by a relative error of at most 0.0031.
Values may be sent and summed in bfloat16 or wider, within the bound.
A program may use at most 64 MiB of HBM per device.

v0:
```python
import jax
import jax.numpy as jnp
from jax import lax
from jax.sharding import PartitionSpec as P


def from_partner(block, axis, distance):
    count = lax.axis_size(axis)
    route = []
    for low in range(count):
        high = low | 1 << distance
        if high != low and high < count:
            route += [(low, high), (high, low)]
    return lax.ppermute(block, axis, route)


def sent_to_all(x, axis):
    copies = jnp.broadcast_to(x, (lax.axis_size(axis), *x.shape))
    return lax.all_to_all(copies, axis, split_axis=0, concat_axis=0, tiled=True)


def all_in_one(x, axis):
    leaves = jax.tree.leaves(x)
    sequence = sorted(range(len(leaves)), key=lambda k: -leaves[k].size)
    width = (1, *leaves[sequence[0]].shape)[-1]
    lines = [
        jnp.pad(leaves[k].reshape(-1), (0, -leaves[k].size % width)).reshape(-1, width)
        for k in sequence
    ]
    both, at, found = (sent_to_all(jnp.concatenate(lines), axis), 0, {})
    for k, line in zip(sequence, lines):
        share = both[:, at : at + len(line)].reshape(len(both), -1)
        found[k] = share[:, : leaves[k].size].reshape(-1, *leaves[k].shape)
        at += len(line)
    numbers = iter(range(len(leaves)))
    return jax.tree.map(lambda _: found[next(numbers)], x)


def joined_by_halves(pieces, combine):
    while len(jax.tree.leaves(pieces)[0]) > 1:
        pieces = jax.vmap(combine)(
            *(jax.tree.map(lambda part: part[side::2], pieces) for side in (0, 1))
        )
    return jax.tree.map(lambda part: part[0], pieces)


def combined_all(x, axis, combine):
    pieces = all_in_one(x, axis)
    return joined_by_halves(pieces, combine)


def cut_along(x, dim, length):
    lengths = x.shape
    tiles = x.reshape(*lengths[:dim], length, lengths[dim] // length, *lengths[dim + 1 :])
    return jnp.moveaxis(tiles, dim, 0)


def sent_and_summed(x, axis, dim):
    length = lax.axis_size(axis)
    tiles = lax.all_to_all(cut_along(x, dim, length), axis, 0, 0, tiled=True)
    return jnp.sum(tiles, axis=0)


def pair_logits(queries, keys_all, factor):
    return factor * lax.dot_general(
        queries, keys_all, (((1,), (1,)), ((), ())), preferred_element_type=jnp.float32
    )


def local_stats(scores):
    column_peak = jnp.max(scores, axis=0)
    return (column_peak, jnp.sum(jnp.exp(scores - column_peak[None, :]), axis=0))


def row_local(scores):
    row_peak = jnp.max(scores, axis=1)
    return (row_peak, jnp.sum(jnp.exp(scores - row_peak[:, None]), axis=1))


def merge_stats(left, right):
    merged = []
    for model_index in range(2):
        peak_left = left[2 * model_index]
        total_left = left[2 * model_index + 1]
        peak_right = right[2 * model_index]
        total_right = right[2 * model_index + 1]
        peak_new = jnp.maximum(peak_left, peak_right)
        merged.append(peak_new)
        merged.append(
            total_left * jnp.exp(peak_left - peak_new)
            + total_right * jnp.exp(peak_right - peak_new)
        )
    return tuple(merged)


def bit_zero(index, bit):
    return index // 2**bit % 2 == 0


def ordered(mine, partner, index, bit):
    return jnp.where(
        bit_zero(index, bit),
        jnp.concatenate([mine, partner], axis=1),
        jnp.concatenate([partner, mine], axis=1),
    )


def halve(block, index, bit, swap_fn):
    half = block.shape[0] // 2
    first = block[:half]
    second = block[half:]
    keep = jnp.where(bit_zero(index, bit), first, second)
    send = jnp.where(bit_zero(index, bit), second, first)
    return keep + swap_fn(send, bit)


def tile_plan(teacher_image, teacher_text, student_image, student_text, scales):
    bits = lax.axis_size("batch").bit_length() - 1
    low_bits = (bits - 1) // 2
    index = lax.axis_index("batch")
    side = lax.axis_index("group")
    top = index // 2 ** (bits - 1) % 2
    own_rows = jnp.stack([teacher_image, student_image])
    other_rows = from_partner(own_rows, "batch", bits - 1)
    row_block = jnp.where(top == side, own_rows, other_rows)
    for bit in range(low_bits):
        partner = from_partner(row_block, "batch", bit)
        row_block = ordered(row_block, partner, index, bit)
    column_block = jnp.stack([teacher_text, student_text])
    for bit in range(low_bits, bits - 1):
        partner = from_partner(column_block, "batch", bit)
        column_block = ordered(column_block, partner, index, bit)
    logits_teacher = pair_logits(row_block[0], column_block[0], scales[0])
    logits_student = pair_logits(row_block[1], column_block[1], scales[1])
    row_state = row_local(logits_teacher) + row_local(logits_student)
    for bit in list(range(low_bits)) + [bits - 1]:
        row_state = merge_stats(row_state, from_partner(row_state, "batch", bit))
    column_state = local_stats(logits_teacher) + local_stats(logits_student)
    for bit in range(low_bits, bits - 1):
        column_state = merge_stats(column_state, from_partner(column_state, "batch", bit))
    column_state = combined_all(column_state, "group", merge_stats)
    row_teacher = row_state[0] + jnp.log(row_state[1])
    row_student = row_state[2] + jnp.log(row_state[3])
    col_teacher = column_state[0] + jnp.log(column_state[1])
    col_student = column_state[2] + jnp.log(column_state[3])
    own_teacher = jnp.exp(logits_teacher - row_teacher[:, None])
    own_student = jnp.exp(logits_student - row_student[:, None])
    other_teacher = jnp.exp(logits_teacher - col_teacher[None, :])
    other_student = jnp.exp(logits_student - col_student[None, :])
    coupling = (0.5 * (own_student - own_teacher + (other_student - other_teacher))).astype(
        jnp.bfloat16
    )
    image_part = scales[1] * jnp.dot(coupling, column_block[1], preferred_element_type=jnp.float32)
    text_part = scales[1] * lax.dot_general(
        coupling, row_block[1], (((0,), (0,)), ((), ())), preferred_element_type=jnp.float32
    )

    def image_swap(send, bit):
        return from_partner(send.astype(jnp.bfloat16), "batch", bit).astype(send.dtype)

    def text_swap(send, bit):
        return from_partner(send.astype(jnp.bfloat16), "batch", bit).astype(send.dtype)

    for bit in reversed(range(low_bits)):
        image_part = halve(image_part, index, bit, image_swap)
    for bit in reversed(range(low_bits, bits - 1)):
        text_part = halve(text_part, index, bit, text_swap)
    image_part = image_part + from_partner(image_part, "batch", bits - 1)
    image_part = jnp.where(top == side, image_part, jnp.zeros_like(image_part))
    return sent_and_summed(jnp.stack([image_part, text_part]), "group", 0)


def per_device(teacher_image, teacher_text, student_image, student_text, scales):
    return tile_plan(teacher_image, teacher_text, student_image, student_text, scales)


def solution(mesh):
    return jax.shard_map(
        per_device,
        mesh=mesh,
        in_specs=(P("batch", None), P("batch", None), P("batch", None), P("batch", None), P()),
        out_specs=P("group", "batch", None),
        check_vma=False,
    )
```

profile of v0, /device:TPU:2, one launch (start us, length us, event | category | flops | bytes accessed | tf_op | source)
XLA Modules:
  0.0 180.9 jit_solution(4960868262526794841)
XLA Ops:
  1.0 2.2 %collective-permute-start = (bf16[2,64,768]{2,1,0:T(8,128)(2,1)S(1)}, bf16[2,64,768]{2,1,0:T(8,128)(2,1)S(1)}, u32[]{:S(2)}, u32[]{:S(2)}) collective-permute-start(bf16[2,64,768]{2,1,0:T(8,128)(2,1)S(1)} %pad_maximum_fusion), channel_id=1, source_target_pairs={{0,64},{64,0},{1,65},{65,1},{2,66},{66,2},{3,67},{67,3},{4,68},{68... | collective-permute-start | bytes 589832 | tf_op jit(solution)/shard_map/ppermute | solution.py:14
  4.1 2.0 %collective-permute-start.4 = (bf16[2,64,768]{2,1,0:T(8,128)(2,1)S(1)}, bf16[2,64,768]{2,1,0:T(8,128)(2,1)S(1)}, u32[]{:S(2)}, u32[]{:S(2)}) collective-permute-start(bf16[2,64,768]{2,1,0:T(8,128)(2,1)S(1)} %pad_maximum_fusion.1), channel_id=1, source_target_pairs={{0,8},{8,0},{1,9},{9,1},{2,10},{10,2},{3,11},{11,3},{4,12},{12,4},... | collective-permute-start | bytes 589832 | tf_op jit(solution)/shard_map/ppermute | solution.py:14
  6.1 3.1 %collective-permute-done = bf16[2,64,768]{2,1,0:T(8,128)(2,1)S(1)} collective-permute-done((bf16[2,64,768]{2,1,0:T(8,128)(2,1)S(1)}, bf16[2,64,768]{2,1,0:T(8,128)(2,1)S(1)}, u32[]{:S(2)}, u32[]{:S(2)}) %collective-permute-start) | collective-permute-done | bytes 196640 | tf_op jit(solution)/shard_map/ppermute | solution.py:14
  11.9 3.4 %collective-permute-start.5 = (bf16[2,128,768]{2,1,0:T(8,128)(2,1)S(1)}, bf16[2,128,768]{2,1,0:T(8,128)(2,1)S(1)}, u32[]{:S(2)}, u32[]{:S(2)}) collective-permute-start(bf16[2,128,768]{2,1,0:T(8,128)(2,1)S(1)} %maximum_select_fusion.5), channel_id=1, source_target_pairs={{0,16},{16,0},{1,17},{17,1},{2,18},{18,2},{3,19},{19,3},{4,20},{20... | collective-permute-start | bytes 1179656 | tf_op jit(solution)/shard_map/ppermute | solution.py:14
  17.0 16.0 %collective-permute-done.5 = bf16[2,128,768]{2,1,0:T(8,128)(2,1)S(1)} collective-permute-done((bf16[2,128,768]{2,1,0:T(8,128)(2,1)S(1)}, bf16[2,128,768]{2,1,0:T(8,128)(2,1)S(1)}, u32[]{:S(2)}, u32[]{:S(2)}) %collective-permute-start.5) | collective-permute-done | bytes 393248 | tf_op jit(solution)/shard_map/ppermute | solution.py:14
  33.3 6.6 %collective-permute-start.6 = (bf16[2,256,768]{2,1,0:T(8,128)(2,1)S(1)}, bf16[2,256,768]{2,1,0:T(8,128)(2,1)S(1)}, u32[]{:S(2)}, u32[]{:S(2)}) collective-permute-start(bf16[2,256,768]{2,1,0:T(8,128)(2,1)S(1)} %maximum_select_fusion.3), channel_id=1, source_target_pairs={{0,32},{32,0},{1,33},{33,1},{2,34},{34,2},{3,35},{35,3},{4,36},{36... | collective-permute-start | bytes 2359304 | tf_op jit(solution)/shard_map/ppermute | solution.py:14
  40.2 3.3 %collective-permute-start.3 = (bf16[2,256,768]{2,1,0:T(8,128)(2,1)S(1)}, bf16[2,256,768]{2,1,0:T(8,128)(2,1)S(1)}, u32[]{:S(2)}, u32[]{:S(2)}) collective-permute-start(bf16[2,256,768]{2,1,0:T(8,128)(2,1)S(1)} %maximum_select_fusion.2), channel_id=1, source_target_pairs={{0,4},{4,0},{1,5},{5,1},{2,6},{6,2},{3,7},{7,3},{8,12},{12,8},{9,1... | collective-permute-start | bytes 2359304 | tf_op jit(solution)/shard_map/ppermute | solution.py:14
  44.2 30.2 %collective-permute-done.6 = bf16[2,256,768]{2,1,0:T(8,128)(2,1)S(1)} collective-permute-done((bf16[2,256,768]{2,1,0:T(8,128)(2,1)S(1)}, bf16[2,256,768]{2,1,0:T(8,128)(2,1)S(1)}, u32[]{:S(2)}, u32[]{:S(2)}) %collective-permute-start.6) | collective-permute-done | bytes 786464 | tf_op jit(solution)/shard_map/ppermute | solution.py:14
  79.7 2.0 %collective-permute-start.29 = (f32[512]{0:T(512)S(1)}, f32[512]{0:T(512)S(1)}, u32[]{:S(2)}, u32[]{:S(2)}) collective-permute-start(f32[512]{0:T(512)S(1)} %get-tuple-element.8), channel_id=1, source_target_pairs={{0,8},{8,0},{1,9},{9,1},{2,10},{10,2},{3,11},{11,3},{4,12},{12,4},... | collective-permute-start | bytes 6152 | tf_op jit(solution)/shard_map/ppermute | solution.py:14
  82.4 3.4 %collective-permute-done.26 = f32[512]{0:T(512)S(1)} collective-permute-done((f32[512]{0:T(512)S(1)}, f32[512]{0:T(512)S(1)}, u32[]{:S(2)}, u32[]{:S(2)}) %collective-permute-start.26) | collective-permute-done | bytes 2080 | tf_op jit(solution)/shard_map/ppermute | solution.py:14
  88.0 3.4 %collective-permute-start.27 = (f32[512]{0:T(512)S(1)}, f32[512]{0:T(512)S(1)}, u32[]{:S(2)}, u32[]{:S(2)}) collective-permute-start(f32[512]{0:T(512)S(1)} %get-tuple-element.29), channel_id=1, source_target_pairs={{0,16},{16,0},{1,17},{17,1},{2,18},{18,2},{3,19},{19,3},{4,20},{20... | collective-permute-start | bytes 6152 | tf_op jit(solution)/shard_map/ppermute | solution.py:14
  91.5 1.7 collective-permute-start.12
  93.7 2.8 %collective-permute-start.33 = (f32[512]{0:T(512)S(1)}, f32[512]{0:T(512)S(1)}, u32[]{:S(2)}, u32[]{:S(2)}) collective-permute-start(f32[512]{0:T(512)S(1)} %get-tuple-element.35), channel_id=1, source_target_pairs={{0,16},{16,0},{1,17},{17,1},{2,18},{18,2},{3,19},{19,3},{4,20},{20... | collective-permute-start | bytes 6152 | tf_op jit(solution)/shard_map/ppermute | solution.py:14
  96.7 3.2 %collective-permute-start.21 = (f32[512]{0:T(512)S(1)}, f32[512]{0:T(512)S(1)}, u32[]{:S(2)}, u32[]{:S(2)}) collective-permute-start(f32[512]{0:T(512)S(1)} %get-tuple-element.21), channel_id=1, source_target_pairs={{0,4},{4,0},{1,5},{5,1},{2,6},{6,2},{3,7},{7,3},{8,12},{12,8},{9,1... | collective-permute-start | bytes 6152 | tf_op jit(solution)/shard_map/ppermute | solution.py:14
  100.4 2.6 %collective-permute-start.28 = (f32[512]{0:T(512)S(1)}, f32[512]{0:T(512)S(1)}, u32[]{:S(2)}, u32[]{:S(2)}) collective-permute-start(f32[512]{0:T(512)S(1)} %get-tuple-element.27), channel_id=1, source_target_pairs={{0,32},{32,0},{1,33},{33,1},{2,34},{34,2},{3,35},{35,3},{4,36},{36... | collective-permute-start | bytes 6152 | tf_op jit(solution)/shard_map/ppermute | solution.py:14
  103.0 3.5 %collective-permute-start.25 = (f32[512]{0:T(512)S(1)}, f32[512]{0:T(512)S(1)}, u32[]{:S(2)}, u32[]{:S(2)}) collective-permute-start(f32[512]{0:T(512)S(1)} %get-tuple-element.28), channel_id=1, source_target_pairs={{0,32},{32,0},{1,33},{33,1},{2,34},{34,2},{3,35},{35,3},{4,36},{36... | collective-permute-start | bytes 6152 | tf_op jit(solution)/shard_map/ppermute | solution.py:14
  106.4 3.2 %collective-permute-start.13 = (f32[512]{0:T(512)S(1)}, f32[512]{0:T(512)S(1)}, u32[]{:S(2)}, u32[]{:S(2)}) collective-permute-start(f32[512]{0:T(512)S(1)} %get-tuple-element.15), channel_id=1, source_target_pairs={{0,4},{4,0},{1,5},{5,1},{2,6},{6,2},{3,7},{7,3},{8,12},{12,8},{9,1... | collective-permute-start | bytes 6152 | tf_op jit(solution)/shard_map/ppermute | solution.py:14
  110.1 2.6 %collective-permute-start.34 = (f32[512]{0:T(512)S(1)}, f32[512]{0:T(512)S(1)}, u32[]{:S(2)}, u32[]{:S(2)}) collective-permute-start(f32[512]{0:T(512)S(1)} %get-tuple-element.33), channel_id=1, source_target_pairs={{0,32},{32,0},{1,33},{33,1},{2,34},{34,2},{3,35},{35,3},{4,36},{36... | collective-permute-start | bytes 6152 | tf_op jit(solution)/shard_map/ppermute | solution.py:14
  112.6 3.5 %collective-permute-start.31 = (f32[512]{0:T(512)S(1)}, f32[512]{0:T(512)S(1)}, u32[]{:S(2)}, u32[]{:S(2)}) collective-permute-start(f32[512]{0:T(512)S(1)} %get-tuple-element.34), channel_id=1, source_target_pairs={{0,32},{32,0},{1,33},{33,1},{2,34},{34,2},{3,35},{35,3},{4,36},{36... | collective-permute-start | bytes 6152 | tf_op jit(solution)/shard_map/ppermute | solution.py:14
  116.1 2.2 %collective-permute-start.22 = (f32[512]{0:T(512)S(1)}, f32[512]{0:T(512)S(1)}, u32[]{:S(2)}, u32[]{:S(2)}) collective-permute-start(f32[512]{0:T(512)S(1)} %get-tuple-element.19), channel_id=1, source_target_pairs={{0,64},{64,0},{1,65},{65,1},{2,66},{66,2},{3,67},{67,3},{4,68},{68... | collective-permute-start | bytes 6152 | tf_op jit(solution)/shard_map/ppermute | solution.py:14
  119.7 2.2 %collective-permute-start.14 = (f32[512]{0:T(512)S(1)}, f32[512]{0:T(512)S(1)}, u32[]{:S(2)}, u32[]{:S(2)}) collective-permute-start(f32[512]{0:T(512)S(1)} %get-tuple-element.13), channel_id=1, source_target_pairs={{0,64},{64,0},{1,65},{65,1},{2,66},{66,2},{3,67},{67,3},{4,68},{68... | collective-permute-start | bytes 6152 | tf_op jit(solution)/shard_map/ppermute | solution.py:14
  124.0 3.7 %all-to-all-start = ((f32[2,4,512]{2,1,0:T(4,128)}), f32[2,4,512]{2,1,0:T(4,128)S(1)}, u32[]{:S(2)}, u32[]{:S(2)}) async-start(f32[2,4,512]{2,1,0:T(4,128)} %broadcast_in_dim.4), calls=%async_computation | async-start | bytes 32768 | tf_op jit(solution)/shard_map/all_to_all | solution.py:19
  127.8 2.0 %all-to-all-done = f32[2,4,512]{2,1,0:T(4,128)S(1)} async-done(((f32[2,4,512]{2,1,0:T(4,128)}), f32[2,4,512]{2,1,0:T(4,128)S(1)}, u32[]{:S(2)}, u32[]{:S(2)}) %all-to-all-start) | async-done | bytes 16416 | tf_op jit(solution)/shard_map/all_to_all | solution.py:19
  132.7 3.3 %collective-permute-start.35 = (bf16[256,768]{1,0:T(8,128)(2,1)S(1)}, bf16[256,768]{1,0:T(8,128)(2,1)S(1)}, u32[]{:S(2)}, u32[]{:S(2)}) collective-permute-start(bf16[256,768]{1,0:T(8,128)(2,1)S(1)} %select_convert_fusion.1), channel_id=1, source_target_pairs={{0,4},{4,0},{1,5},{5,1},{2,6},{6,2},{3,7},{7,3},{8,12},{12,8},{9,1... | collective-permute-start | bytes 1179656 | tf_op jit(solution)/shard_map/ppermute | solution.py:14
  137.3 2.6 %collective-permute-start.39 = (bf16[256,768]{1,0:T(8,128)(2,1)S(1)}, bf16[256,768]{1,0:T(8,128)(2,1)S(1)}, u32[]{:S(2)}, u32[]{:S(2)}) collective-permute-start(bf16[256,768]{1,0:T(8,128)(2,1)S(1)} %select_convert_fusion), channel_id=1, source_target_pairs={{0,32},{32,0},{1,33},{33,1},{2,34},{34,2},{3,35},{35,3},{4,36},{36... | collective-permute-start | bytes 1179656 | tf_op jit(solution)/shard_map/ppermute | solution.py:14
  140.0 4.2 %collective-permute-done.35 = bf16[256,768]{1,0:T(8,128)(2,1)S(1)} collective-permute-done((bf16[256,768]{1,0:T(8,128)(2,1)S(1)}, bf16[256,768]{1,0:T(8,128)(2,1)S(1)}, u32[]{:S(2)}, u32[]{:S(2)}) %collective-permute-start.35) | collective-permute-done | bytes 393248 | tf_op jit(solution)/shard_map/ppermute | solution.py:14
  145.2 11.8 %collective-permute-done.39 = bf16[256,768]{1,0:T(8,128)(2,1)S(1)} collective-permute-done((bf16[256,768]{1,0:T(8,128)(2,1)S(1)}, bf16[256,768]{1,0:T(8,128)(2,1)S(1)}, u32[]{:S(2)}, u32[]{:S(2)}) %collective-permute-start.39) | collective-permute-done | bytes 393248 | tf_op jit(solution)/shard_map/ppermute | solution.py:14
  157.5 6.4 %collective-permute-done.40 = bf16[128,768]{1,0:T(8,128)(2,1)S(1)} collective-permute-done((bf16[128,768]{1,0:T(8,128)(2,1)S(1)}, bf16[128,768]{1,0:T(8,128)(2,1)S(1)}, u32[]{:S(2)}, u32[]{:S(2)}) %collective-permute-start.40) | collective-permute-done | bytes 196640 | tf_op jit(solution)/shard_map/ppermute | solution.py:14
  164.1 2.8 %collective-permute-start.38 = (f32[64,768]{1,0:T(8,128)S(1)}, f32[64,768]{1,0:T(8,128)S(1)}, u32[]{:S(2)}, u32[]{:S(2)}) collective-permute-start(f32[64,768]{1,0:T(8,128)S(1)} %convert_add_fusion.4), channel_id=1, source_target_pairs={{0,64},{64,0},{1,65},{65,1},{2,66},{66,2},{3,67},{67,3},{4,68},{68... | collective-permute-start | bytes 589832 | tf_op jit(solution)/shard_map/ppermute | solution.py:14
  166.9 1.7 collective-permute-done.41
  168.7 2.7 %collective-permute-done.38 = f32[64,768]{1,0:T(8,128)S(1)} collective-permute-done((f32[64,768]{1,0:T(8,128)S(1)}, f32[64,768]{1,0:T(8,128)S(1)}, u32[]{:S(2)}, u32[]{:S(2)}) %collective-permute-start.38) | collective-permute-done | bytes 196640 | tf_op jit(solution)/shard_map/ppermute | solution.py:14
  171.4 8.7 %all_to_all.10 = f32[2,1,64,768]{3,2,1,0:T(8,128)S(1)} all-to-all(f32[2,1,64,768]{3,2,1,0:T(8,128)S(1)} %maximum_bitcast_fusion), channel_id=1, replica_groups=mesh['group'=2,'batch'=128] {'group'}, dimensions={0} | all-to-all | bytes 786432 | tf_op jit(solution)/shard_map/all_to_all | solution.py:60
  (115 shorter events, 27.6 us)
Async XLA Ops:
  1.0 8.2 %collective-permute-start = (bf16[2,64,768]{2,1,0:T(8,128)(2,1)S(1)}, bf16[2,64,768]{2,1,0:T(8,128)(2,1)S(1)}, u32[]{:S(2)}, u32[]{:S(2)}) collective-permute-start(bf16[2,64,768]{2,1,0:T(8,128)(2,1)S(1)} %pad_maximum_fusion), channel_id=1, source_target_pairs={{0,64},{64,0},{1,65},{65,1},{2,66},{66,2},{3,67},{67,3},{4,68},{68... | collective-permute-start | bytes 589832 | tf_op jit(solution)/shard_map/ppermute | solution.py:14
  4.1 6.6 %collective-permute-start.4 = (bf16[2,64,768]{2,1,0:T(8,128)(2,1)S(1)}, bf16[2,64,768]{2,1,0:T(8,128)(2,1)S(1)}, u32[]{:S(2)}, u32[]{:S(2)}) collective-permute-start(bf16[2,64,768]{2,1,0:T(8,128)(2,1)S(1)} %pad_maximum_fusion.1), channel_id=1, source_target_pairs={{0,8},{8,0},{1,9},{9,1},{2,10},{10,2},{3,11},{11,3},{4,12},{12,4},... | collective-permute-start | bytes 589832 | tf_op jit(solution)/shard_map/ppermute | solution.py:14
  11.9 21.1 %collective-permute-start.5 = (bf16[2,128,768]{2,1,0:T(8,128)(2,1)S(1)}, bf16[2,128,768]{2,1,0:T(8,128)(2,1)S(1)}, u32[]{:S(2)}, u32[]{:S(2)}) collective-permute-start(bf16[2,128,768]{2,1,0:T(8,128)(2,1)S(1)} %maximum_select_fusion.5), channel_id=1, source_target_pairs={{0,16},{16,0},{1,17},{17,1},{2,18},{18,2},{3,19},{19,3},{4,20},{20... | collective-permute-start | bytes 1179656 | tf_op jit(solution)/shard_map/ppermute | solution.py:14
  15.3 24.6 %collective-permute-start.2 = (bf16[2,128,768]{2,1,0:T(8,128)(2,1)S(1)}, bf16[2,128,768]{2,1,0:T(8,128)(2,1)S(1)}, u32[]{:S(2)}, u32[]{:S(2)}) collective-permute-start(bf16[2,128,768]{2,1,0:T(8,128)(2,1)S(1)} %maximum_select_fusion.4), channel_id=1, source_target_pairs={{0,2},{2,0},{1,3},{3,1},{4,6},{6,4},{5,7},{7,5},{8,10},{10,8},{9,1... | collective-permute-start | bytes 1179656 | tf_op jit(solution)/shard_map/ppermute | solution.py:14
  33.3 41.1 %collective-permute-start.6 = (bf16[2,256,768]{2,1,0:T(8,128)(2,1)S(1)}, bf16[2,256,768]{2,1,0:T(8,128)(2,1)S(1)}, u32[]{:S(2)}, u32[]{:S(2)}) collective-permute-start(bf16[2,256,768]{2,1,0:T(8,128)(2,1)S(1)} %maximum_select_fusion.3), channel_id=1, source_target_pairs={{0,32},{32,0},{1,33},{33,1},{2,34},{34,2},{3,35},{35,3},{4,36},{36... | collective-permute-start | bytes 2359304 | tf_op jit(solution)/shard_map/ppermute | solution.py:14
  40.2 34.9 %collective-permute-start.3 = (bf16[2,256,768]{2,1,0:T(8,128)(2,1)S(1)}, bf16[2,256,768]{2,1,0:T(8,128)(2,1)S(1)}, u32[]{:S(2)}, u32[]{:S(2)}) collective-permute-start(bf16[2,256,768]{2,1,0:T(8,128)(2,1)S(1)} %maximum_select_fusion.2), channel_id=1, source_target_pairs={{0,4},{4,0},{1,5},{5,1},{2,6},{6,2},{3,7},{7,3},{8,12},{12,8},{9,1... | collective-permute-start | bytes 2359304 | tf_op jit(solution)/shard_map/ppermute | solution.py:14
  77.2 8.6 %collective-permute-start.23 = (f32[512]{0:T(512)S(1)}, f32[512]{0:T(512)S(1)}, u32[]{:S(2)}, u32[]{:S(2)}) collective-permute-start(f32[512]{0:T(512)S(1)} %get-tuple-element.12), channel_id=1, source_target_pairs={{0,8},{8,0},{1,9},{9,1},{2,10},{10,2},{3,11},{11,3},{4,12},{12,4},... | collective-permute-start | bytes 6152 | tf_op jit(solution)/shard_map/ppermute | solution.py:14
  79.6 8.4 %collective-permute-start.7 = (f32[512]{0:T(512)S(1)}, f32[512]{0:T(512)S(1)}, u32[]{:S(2)}, u32[]{:S(2)}) collective-permute-start(f32[512]{0:T(512)S(1)} %get-tuple-element.7), channel_id=1, source_target_pairs={{0,1},{1,0},{2,3},{3,2},{4,5},{5,4},{6,7},{7,6},{8,9},{9,8},{10,11... | collective-permute-start | bytes 6152 | tf_op jit(solution)/shard_map/ppermute | solution.py:14
  79.7 11.7 %collective-permute-start.29 = (f32[512]{0:T(512)S(1)}, f32[512]{0:T(512)S(1)}, u32[]{:S(2)}, u32[]{:S(2)}) collective-permute-start(f32[512]{0:T(512)S(1)} %get-tuple-element.8), channel_id=1, source_target_pairs={{0,8},{8,0},{1,9},{9,1},{2,10},{10,2},{3,11},{11,3},{4,12},{12,4},... | collective-permute-start | bytes 6152 | tf_op jit(solution)/shard_map/ppermute | solution.py:14
  85.8 7.3 %collective-permute-start.20 = (f32[512]{0:T(512)S(1)}, f32[512]{0:T(512)S(1)}, u32[]{:S(2)}, u32[]{:S(2)}) collective-permute-start(f32[512]{0:T(512)S(1)} %get-tuple-element.23), channel_id=1, source_target_pairs={{0,2},{2,0},{1,3},{3,1},{4,6},{6,4},{5,7},{7,5},{8,10},{10,8},{9,1... | collective-permute-start | bytes 6152 | tf_op jit(solution)/shard_map/ppermute | solution.py:14
  87.5 6.3 %collective-permute-start.16 = (f32[512]{0:T(512)S(1)}, f32[512]{0:T(512)S(1)}, u32[]{:S(2)}, u32[]{:S(2)}) collective-permute-start(f32[512]{0:T(512)S(1)} %get-tuple-element.24), channel_id=1, source_target_pairs={{0,2},{2,0},{1,3},{3,1},{4,6},{6,4},{5,7},{7,5},{8,10},{10,8},{9,1... | collective-permute-start | bytes 6152 | tf_op jit(solution)/shard_map/ppermute | solution.py:14
  88.0 8.6 %collective-permute-start.27 = (f32[512]{0:T(512)S(1)}, f32[512]{0:T(512)S(1)}, u32[]{:S(2)}, u32[]{:S(2)}) collective-permute-start(f32[512]{0:T(512)S(1)} %get-tuple-element.29), channel_id=1, source_target_pairs={{0,16},{16,0},{1,17},{17,1},{2,18},{18,2},{3,19},{19,3},{4,20},{20... | collective-permute-start | bytes 6152 | tf_op jit(solution)/shard_map/ppermute | solution.py:14
  91.5 8.5 %collective-permute-start.12 = (f32[512]{0:T(512)S(1)}, f32[512]{0:T(512)S(1)}, u32[]{:S(2)}, u32[]{:S(2)}) collective-permute-start(f32[512]{0:T(512)S(1)} %get-tuple-element.17), channel_id=1, source_target_pairs={{0,2},{2,0},{1,3},{3,1},{4,6},{6,4},{5,7},{7,5},{8,10},{10,8},{9,1... | collective-permute-start | bytes 6152 | tf_op jit(solution)/shard_map/ppermute | solution.py:14
  93.2 7.2 %collective-permute-start.8 = (f32[512]{0:T(512)S(1)}, f32[512]{0:T(512)S(1)}, u32[]{:S(2)}, u32[]{:S(2)}) collective-permute-start(f32[512]{0:T(512)S(1)} %get-tuple-element.18), channel_id=1, source_target_pairs={{0,2},{2,0},{1,3},{3,1},{4,6},{6,4},{5,7},{7,5},{8,10},{10,8},{9,1... | collective-permute-start | bytes 6152 | tf_op jit(solution)/shard_map/ppermute | solution.py:14
  93.7 9.2 %collective-permute-start.33 = (f32[512]{0:T(512)S(1)}, f32[512]{0:T(512)S(1)}, u32[]{:S(2)}, u32[]{:S(2)}) collective-permute-start(f32[512]{0:T(512)S(1)} %get-tuple-element.35), channel_id=1, source_target_pairs={{0,16},{16,0},{1,17},{17,1},{2,18},{18,2},{3,19},{19,3},{4,20},{20... | collective-permute-start | bytes 6152 | tf_op jit(solution)/shard_map/ppermute | solution.py:14
  96.5 9.9 %collective-permute-start.30 = (f32[512]{0:T(512)S(1)}, f32[512]{0:T(512)S(1)}, u32[]{:S(2)}, u32[]{:S(2)}) collective-permute-start(f32[512]{0:T(512)S(1)} %get-tuple-element.36), channel_id=1, source_target_pairs={{0,16},{16,0},{1,17},{17,1},{2,18},{18,2},{3,19},{19,3},{4,20},{20... | collective-permute-start | bytes 6152 | tf_op jit(solution)/shard_map/ppermute | solution.py:14
  96.7 12.9 %collective-permute-start.21 = (f32[512]{0:T(512)S(1)}, f32[512]{0:T(512)S(1)}, u32[]{:S(2)}, u32[]{:S(2)}) collective-permute-start(f32[512]{0:T(512)S(1)} %get-tuple-element.21), channel_id=1, source_target_pairs={{0,4},{4,0},{1,5},{5,1},{2,6},{6,2},{3,7},{7,3},{8,12},{12,8},{9,1... | collective-permute-start | bytes 6152 | tf_op jit(solution)/shard_map/ppermute | solution.py:14
  100.0 10.1 %collective-permute-start.17 = (f32[512]{0:T(512)S(1)}, f32[512]{0:T(512)S(1)}, u32[]{:S(2)}, u32[]{:S(2)}) collective-permute-start(f32[512]{0:T(512)S(1)} %get-tuple-element.22), channel_id=1, source_target_pairs={{0,4},{4,0},{1,5},{5,1},{2,6},{6,2},{3,7},{7,3},{8,12},{12,8},{9,1... | collective-permute-start | bytes 6152 | tf_op jit(solution)/shard_map/ppermute | solution.py:14
  100.4 17.9 %collective-permute-start.28 = (f32[512]{0:T(512)S(1)}, f32[512]{0:T(512)S(1)}, u32[]{:S(2)}, u32[]{:S(2)}) collective-permute-start(f32[512]{0:T(512)S(1)} %get-tuple-element.27), channel_id=1, source_target_pairs={{0,32},{32,0},{1,33},{33,1},{2,34},{34,2},{3,35},{35,3},{4,36},{36... | collective-permute-start | bytes 6152 | tf_op jit(solution)/shard_map/ppermute | solution.py:14
  103.0 16.8 %collective-permute-start.25 = (f32[512]{0:T(512)S(1)}, f32[512]{0:T(512)S(1)}, u32[]{:S(2)}, u32[]{:S(2)}) collective-permute-start(f32[512]{0:T(512)S(1)} %get-tuple-element.28), channel_id=1, source_target_pairs={{0,32},{32,0},{1,33},{33,1},{2,34},{34,2},{3,35},{35,3},{4,36},{36... | collective-permute-start | bytes 6152 | tf_op jit(solution)/shard_map/ppermute | solution.py:14
  109.6 6.5 %collective-permute-start.9 = (f32[512]{0:T(512)S(1)}, f32[512]{0:T(512)S(1)}, u32[]{:S(2)}, u32[]{:S(2)}) collective-permute-start(f32[512]{0:T(512)S(1)} %get-tuple-element.16), channel_id=1, source_target_pairs={{0,4},{4,0},{1,5},{5,1},{2,6},{6,2},{3,7},{7,3},{8,12},{12,8},{9,1... | collective-permute-start | bytes 6152 | tf_op jit(solution)/shard_map/ppermute | solution.py:14
  110.1 11.8 %collective-permute-start.34 = (f32[512]{0:T(512)S(1)}, f32[512]{0:T(512)S(1)}, u32[]{:S(2)}, u32[]{:S(2)}) collective-permute-start(f32[512]{0:T(512)S(1)} %get-tuple-element.33), channel_id=1, source_target_pairs={{0,32},{32,0},{1,33},{33,1},{2,34},{34,2},{3,35},{35,3},{4,36},{36... | collective-permute-start | bytes 6152 | tf_op jit(solution)/shard_map/ppermute | solution.py:14
  112.6 10.7 %collective-permute-start.31 = (f32[512]{0:T(512)S(1)}, f32[512]{0:T(512)S(1)}, u32[]{:S(2)}, u32[]{:S(2)}) collective-permute-start(f32[512]{0:T(512)S(1)} %get-tuple-element.34), channel_id=1, source_target_pairs={{0,32},{32,0},{1,33},{33,1},{2,34},{34,2},{3,35},{35,3},{4,36},{36... | collective-permute-start | bytes 6152 | tf_op jit(solution)/shard_map/ppermute | solution.py:14
  116.1 11.7 %collective-permute-start.22 = (f32[512]{0:T(512)S(1)}, f32[512]{0:T(512)S(1)}, u32[]{:S(2)}, u32[]{:S(2)}) collective-permute-start(f32[512]{0:T(512)S(1)} %get-tuple-element.19), channel_id=1, source_target_pairs={{0,64},{64,0},{1,65},{65,1},{2,66},{66,2},{3,67},{67,3},{4,68},{68... | collective-permute-start | bytes 6152 | tf_op jit(solution)/shard_map/ppermute | solution.py:14
  118.3 9.5 %collective-permute-start.18 = (f32[512]{0:T(512)S(1)}, f32[512]{0:T(512)S(1)}, u32[]{:S(2)}, u32[]{:S(2)}) collective-permute-start(f32[512]{0:T(512)S(1)} %get-tuple-element.20), channel_id=1, source_target_pairs={{0,64},{64,0},{1,65},{65,1},{2,66},{66,2},{3,67},{67,3},{4,68},{68... | collective-permute-start | bytes 6152 | tf_op jit(solution)/shard_map/ppermute | solution.py:14
  119.7 8.0 %collective-permute-start.14 = (f32[512]{0:T(512)S(1)}, f32[512]{0:T(512)S(1)}, u32[]{:S(2)}, u32[]{:S(2)}) collective-permute-start(f32[512]{0:T(512)S(1)} %get-tuple-element.13), channel_id=1, source_target_pairs={{0,64},{64,0},{1,65},{65,1},{2,66},{66,2},{3,67},{67,3},{4,68},{68... | collective-permute-start | bytes 6152 | tf_op jit(solution)/shard_map/ppermute | solution.py:14
  132.7 11.5 %collective-permute-start.35 = (bf16[256,768]{1,0:T(8,128)(2,1)S(1)}, bf16[256,768]{1,0:T(8,128)(2,1)S(1)}, u32[]{:S(2)}, u32[]{:S(2)}) collective-permute-start(bf16[256,768]{1,0:T(8,128)(2,1)S(1)} %select_convert_fusion.1), channel_id=1, source_target_pairs={{0,4},{4,0},{1,5},{5,1},{2,6},{6,2},{3,7},{7,3},{8,12},{12,8},{9,1... | collective-permute-start | bytes 1179656 | tf_op jit(solution)/shard_map/ppermute | solution.py:14
  137.3 19.7 %collective-permute-start.39 = (bf16[256,768]{1,0:T(8,128)(2,1)S(1)}, bf16[256,768]{1,0:T(8,128)(2,1)S(1)}, u32[]{:S(2)}, u32[]{:S(2)}) collective-permute-start(bf16[256,768]{1,0:T(8,128)(2,1)S(1)} %select_convert_fusion), channel_id=1, source_target_pairs={{0,32},{32,0},{1,33},{33,1},{2,34},{34,2},{3,35},{35,3},{4,36},{36... | collective-permute-start | bytes 1179656 | tf_op jit(solution)/shard_map/ppermute | solution.py:14
  144.3 12.9 %collective-permute-start.36 = (bf16[128,768]{1,0:T(8,128)(2,1)S(1)}, bf16[128,768]{1,0:T(8,128)(2,1)S(1)}, u32[]{:S(2)}, u32[]{:S(2)}) collective-permute-start(bf16[128,768]{1,0:T(8,128)(2,1)S(1)} %select_convert_fusion.3), channel_id=1, source_target_pairs={{0,2},{2,0},{1,3},{3,1},{4,6},{6,4},{5,7},{7,5},{8,10},{10,8},{9,1... | collective-permute-start | bytes 589832 | tf_op jit(solution)/shard_map/ppermute | solution.py:14
  157.2 6.7 %collective-permute-start.40 = (bf16[128,768]{1,0:T(8,128)(2,1)S(1)}, bf16[128,768]{1,0:T(8,128)(2,1)S(1)}, u32[]{:S(2)}, u32[]{:S(2)}) collective-permute-start(bf16[128,768]{1,0:T(8,128)(2,1)S(1)} %select_convert_fusion.2), channel_id=1, source_target_pairs={{0,16},{16,0},{1,17},{17,1},{2,18},{18,2},{3,19},{19,3},{4,20},{20... | collective-permute-start | bytes 589832 | tf_op jit(solution)/shard_map/ppermute | solution.py:14
  157.4 6.7 %collective-permute-start.37 = (bf16[64,768]{1,0:T(8,128)(2,1)S(1)}, bf16[64,768]{1,0:T(8,128)(2,1)S(1)}, u32[]{:S(2)}, u32[]{:S(2)}) collective-permute-start(bf16[64,768]{1,0:T(8,128)(2,1)S(1)} %select_convert_fusion.5), channel_id=1, source_target_pairs={{0,1},{1,0},{2,3},{3,2},{4,5},{5,4},{6,7},{7,6},{8,9},{9,8},{10,11... | collective-permute-start | bytes 294920 | tf_op jit(solution)/shard_map/ppermute | solution.py:14
  164.1 7.3 %collective-permute-start.38 = (f32[64,768]{1,0:T(8,128)S(1)}, f32[64,768]{1,0:T(8,128)S(1)}, u32[]{:S(2)}, u32[]{:S(2)}) collective-permute-start(f32[64,768]{1,0:T(8,128)S(1)} %convert_add_fusion.4), channel_id=1, source_target_pairs={{0,64},{64,0},{1,65},{65,1},{2,66},{66,2},{3,67},{67,3},{4,68},{68... | collective-permute-start | bytes 589832 | tf_op jit(solution)/shard_map/ppermute | solution.py:14
  (16 other events, 95.3 us)
where the time goes:
time: 184 us; the launch traced here: 181 us
  waiting for transfers between devices  82.1 us (45%)
  starting transfers between devices  73.3 us (40%)
  other arithmetic  8.93 us (5%)
  blocking collectives  8.75 us (5%)
  matrix products  5.4 us (3%)
  local copies, waits for them, and re-layouts  2.06 us (1%)
    ppermute x42, waiting for transfers between devices, from_partner(): return lax.ppermute(block, axis, route)  80.1 us
    ppermute x42, starting transfers between devices, from_partner(): return lax.ppermute(block, axis, route)  69.5 us
    all_to_all x1, blocking collectives, sent_and_summed(): tiles = lax.all_to_all(cut_along(x, dim, length), axis, 0, 0, tiled=True)  8.75 us
    all_to_all x1, starting transfers between devices, sent_to_all(): return lax.all_to_all(copies, axis, split_axis=0, concat_axis=0, tiled=True)  3.74 us
  transfers between devices with their start and end apart: 43, of which 11 were waited for; matrix products, arithmetic and copies ran while one was open for 5% of the time, Pallas kernels for 0%

commit v1 on v0

v1 whole, which is shorter than its diff:
```python
import jax
import jax.numpy as jnp
from jax import lax
from jax.experimental import pallas as pl
from jax.experimental.pallas import tpu as pltpu
from jax.sharding import PartitionSpec as P

MESH = pl.DeviceIdType.MESH
F32 = jnp.float32
BF16 = jnp.bfloat16
NX, NY, NZ, NC = 4, 4, 8, 2
N = 64
ROWS = NZ * N
COLS = NY * 2 * N
SENDS = 80


def device(x_hi, x_lo, y, z, core):
    return {"group": x_lo, "batch": ((x_hi * NZ + z) * NY + y) * NC + core}


def kernel(
    ti, tt, si, st, scales, out,
    rows, cols, logits, rowst, stat, rstat, cstat, rcol, cpl, cplt,
    tacc, tsend, arecv, brecv, xsend, xrecv, isend, iown, irecv, zsend, zrecv, fsend, frecv,
    lsem, ssem, rsem, csem, rssem, cssem, asem, bsem, xsem, isem, zsem, fsem,
):
    width = ti.shape[1]
    b = lax.axis_index("batch")
    g = lax.axis_index("group")
    core, y, z, xh = b % NC, (b // NC) % NY, (b // (NC * NY)) % NZ, b // (NC * NY * NZ)
    x = 2 * xh + g
    other = 1 - core
    step = 1 - 2 * core
    yu, yd, y2 = (y + 1) % NY, (y + 3) % NY, (y + 2) % NY
    source = core == g

    sibling = device(xh, g, y, z, other)
    up_y, down_y = device(xh, g, yu, z, core), device(xh, g, yd, z, core)
    across = device(1 - xh, 1 - g, y, z, core)
    beside = device(xh, 1 - g, y, z, core)
    along = device(xh, g, y, (z + step + NZ) % NZ, core)

    pending = []

    def copy(src, dst, sem, to):
        k = len(pending)
        c = pltpu.make_async_remote_copy(
            src_ref=src, dst_ref=dst, send_sem=ssem.at[k], recv_sem=sem, device_id=to, device_id_type=MESH
        )
        return c

    def send(src, dst, sem, to, when=None):
        c = copy(src, dst, sem, to)
        pending.append((c, when))
        if when is None:
            c.start()
        else:
            pl.when(when)(c.start)

    def arrived(dst, sem):
        pltpu.make_async_remote_copy(
            src_ref=dst, dst_ref=dst, send_sem=ssem.at[SENDS - 1], recv_sem=sem, device_id=sibling, device_id_type=MESH
        ).wait_recv()

    def row_at(m, k):
        return rows.at[m, pl.ds(pl.multiple_of(k * N, N), N)]

    def col_slot(yy, hi):
        return yy * 2 + hi

    def col_at(m, k):
        return cols.at[m, pl.ds(pl.multiple_of(k * N, N), N)]

    mine = col_slot(y, xh)
    locals_ = [
        pltpu.make_async_copy(tt, col_at(0, mine), lsem.at[0]),
        pltpu.make_async_copy(st, col_at(1, mine), lsem.at[1]),
    ]
    row_locals = [
        pltpu.make_async_copy(ti, row_at(0, z), lsem.at[2]),
        pltpu.make_async_copy(si, row_at(1, z), lsem.at[3]),
    ]
    for c in locals_:
        c.start()

    @pl.when(source)
    def _():
        for c in row_locals:
            c.start()

    row_me, col_me = z * NC + core, x * NY + y

    def row_peer(j):
        q = (row_me + j) % (NZ * NC)
        return q, device(xh, g, y, q // NC, q % NC)

    def col_peer(j):
        q = (col_me + j) % (NX * NY)
        qx = q // NY
        return q, device(qx // 2, qx % 2, q % NY, z, core)

    barrier = pltpu.get_barrier_semaphore()

    @pl.loop(1, 16)
    def _(j):
        pl.semaphore_signal(barrier, inc=1, device_id=row_peer(j)[1], device_id_type=MESH)
        pl.semaphore_signal(barrier, inc=1, device_id=col_peer(j)[1], device_id_type=MESH)

    pl.semaphore_wait(barrier, 30)
    for c in locals_:
        c.wait()

    @pl.when(source)
    def _():
        for c in row_locals:
            c.wait()

    m1, m2 = g, 1 - g

    def send_col(m, k, to, when=None):
        send(col_at(m, k), col_at(m, k), csem.at[m, k], to, when)

    def send_row(m, k, to, when=None):
        send(row_at(m, k), row_at(m, k), rsem.at[m, k], to, when)

    def got_col(m, k):
        arrived(col_at(m, k), csem.at[m, k])

    def got_row(m, k):
        arrived(row_at(m, k), rsem.at[m, k])

    zu, zd = (z + 1) % NZ, (z + NZ - 1) % NZ
    send_col(m1, mine, across)
    send_col(m1, mine, up_y)
    send_col(m1, mine, down_y)
    for m in (0, 1):
        send_row(m, z, device(xh, g, y, zu, 0), source)
        send_row(m, z, device(xh, g, y, zd, 1), source)
    send_col(m2, mine, up_y)
    send_col(m2, mine, down_y)
    for m in (0, 1):
        send_row(m, z, sibling, source)

    def z_hop(d, models, onward):
        k = (z - step * d + NZ) % NZ
        for m in models:
            got_row(m, k)
            if onward == "all":
                send_row(m, k, along)
            send_row(m, k, sibling)
        if onward == "own":
            send_row(core, k, along)

    def x_hop(yy):
        k = col_slot(yy, 1 - xh)
        got_col(m2, k)
        send_col(m2, k, beside)

    def y_slot(yy):
        return col_slot(yy, xh)

    z_hop(1, (0, 1), "all")
    x_hop(y)
    got_col(m1, y_slot(yd))
    send_col(m1, y_slot(yd), up_y)
    send_col(m1, y_slot(yd), across)
    got_col(m1, y_slot(yu))
    send_col(m1, y_slot(yu), across)
    z_hop(2, (0, 1), "all")
    got_col(m2, y_slot(yu))
    send_col(m2, y_slot(yu), down_y)
    got_col(m2, y_slot(yd))
    x_hop(yd)
    x_hop(yu)
    z_hop(3, (0, 1), "own")
    got_col(m1, y_slot(y2))
    send_col(m1, y_slot(y2), across)
    got_col(m2, y_slot(y2))
    z_hop(4, (core,), None)
    x_hop(y2)
    for d in (1, 2, 3):
        for m in (0, 1):
            got_row(m, (z + step * d + NZ) % NZ)
    got_row(other, (z + 4) % NZ)

    @pl.when(jnp.logical_not(source))
    def _():
        for m in (0, 1):
            got_row(m, z)

    for yy in (y, yd, yu, y2):
        got_col(m1, col_slot(yy, 1 - xh))

    for m in (0, 1):
        factor = scales[m]

        @pl.loop(0, ROWS // 256)
        def _(i):
            block = pl.ds(pl.multiple_of(i * 256, 256), 256)
            logits[m, block, :] = factor * lax.dot_general(
                rows[m, block, :], cols[m], (((1,), (1,)), ((), ())), preferred_element_type=F32
            )

    lane = lax.broadcasted_iota(jnp.int32, (N, 128), 1)
    rowst[...] = jnp.zeros_like(rowst)
    for m in (0, 1):

        def local(i, state):
            peak, total = state
            l = logits[m, pl.ds(pl.multiple_of(i * N, N), N), :]
            row_peak = jnp.max(l, axis=1, keepdims=True)
            row_lse = row_peak + jnp.log(jnp.sum(jnp.exp(l - row_peak), axis=1, keepdims=True))
            half = pl.ds(pl.multiple_of((i % 2) * N, N), N)
            rowst[half, :] = jnp.where(lane == 4 * m + i // 2, row_lse, rowst[half, :])
            now = jnp.maximum(peak, jnp.max(l, axis=0, keepdims=True))
            total = total * jnp.exp(peak - now) + jnp.sum(jnp.exp(l - now), axis=0, keepdims=True)
            return now, total

        start = (jnp.full((1, COLS), -3.0e38, F32), jnp.zeros((1, COLS), F32))
        peak, total = lax.fori_loop(0, ROWS // N, local, start)
        col_lse = peak + jnp.log(total)
        for i in range(COLS // 128):
            stat[4 * m + i : 4 * m + i + 1, :] = col_lse[:, 128 * i : 128 * (i + 1)]

    cstat[col_me] = stat[...]
    rstat[row_me] = rowst[...].T[:8, :]
    sent = len(pending)

    def stat_copy(kind, j):
        if kind == 0:
            q, to = row_peer(j)
            return pltpu.make_async_remote_copy(
                src_ref=rstat.at[row_me], dst_ref=rstat.at[row_me], send_sem=ssem.at[sent + j], recv_sem=rssem.at[row_me],
                device_id=to, device_id_type=MESH,
            ), q
        q, to = col_peer(j)
        return pltpu.make_async_remote_copy(
            src_ref=cstat.at[col_me], dst_ref=cstat.at[col_me], send_sem=cssend(j), recv_sem=cssem.at[col_me],
            device_id=to, device_id_type=MESH,
        ), q

    def cssend(j):
        return ssem.at[SENDS + j]

    @pl.loop(1, 16)
    def _(j):
        stat_copy(0, j)[0].start()
        stat_copy(1, j)[0].start()

    @pl.loop(1, 16)
    def _(j):
        q = row_peer(j)[0]
        arrived(rstat.at[q], rssem.at[q])
        q = col_peer(j)[0]
        arrived(cstat.at[q], cssem.at[q])

    @pl.loop(1, 16)
    def _(j):
        stat_copy(0, j)[0].wait_send()
        stat_copy(1, j)[0].wait_send()

    pending.extend([None] * 16)

    def joined(all_):
        peak = jnp.max(all_, axis=0)
        return peak + jnp.log(jnp.sum(jnp.exp(all_ - peak[None]), axis=0))

    stat[...] = joined(cstat[...])
    rowst[0:8, :] = joined(rstat[...])
    turned = rowst[...].T
    for m in (0, 1):
        for i in range(ROWS // 128):
            rcol[m, 128 * i : 128 * (i + 1), :] = jnp.broadcast_to(turned[:, 4 * m + i : 4 * m + i + 1], (128, 128))
    col_lse = [
        jnp.concatenate([stat[4 * m + i : 4 * m + i + 1, :] for i in range(COLS // 128)], axis=1) for m in (0, 1)
    ]

    @pl.loop(0, ROWS // 128)
    def _(i):
        block = pl.ds(pl.multiple_of(i * 128, 128), 128)
        terms = []
        for m in (0, 1):
            l = logits[m, block, :]
            r = jnp.concatenate([rcol[m, block, :]] * (COLS // 128), axis=1)
            terms.append((jnp.exp(l - r), jnp.exp(l - col_lse[m])))
        c = 0.5 * ((terms[1][0] - terms[0][0]) + (terms[1][1] - terms[0][1]))
        cpl[block, :] = c.astype(BF16)
        cplt[:, block] = c.T.astype(BF16)

    factor = scales[1]

    def text_dot(ya, yb):
        a = jnp.concatenate([cplt[pl.ds(pl.multiple_of(k * 128, 128), 128), :] for k in (ya, yb)], axis=0)
        return factor * jnp.dot(a, rows[1], preferred_element_type=F32)

    def image_dot(first):
        parts = [(z + first + k) % NZ for k in range(4)]
        a = jnp.concatenate([cpl[pl.ds(pl.multiple_of(k * N, N), N), :] for k in parts], axis=0)
        return factor * jnp.dot(a, cols[1], preferred_element_type=F32)

    far = text_dot(y2, yu)
    tacc[0:256, :] = far
    tsend[0:128, :] = far[0:128].astype(BF16)
    send(tsend.at[pl.ds(0, N)], arecv.at[0], asem.at[0], up_y)
    send(tsend.at[pl.ds(N, N)], arecv.at[1], asem.at[1], down_y)
    first = 4 * ((core + g) % 2)
    isend[...] = image_dot(4 - first).astype(BF16)
    send(isend, irecv, isem.at[0], sibling)
    tacc[256:512, :] = text_dot(yd, y)
    arrived(arecv.at[0], asem.at[0])
    tsend[128:192, :] = (tacc[128:192, :] + arecv[0].astype(F32)).astype(BF16)
    tsend[192:256, :] = tacc[192:256, :].astype(BF16)
    send(tsend.at[pl.ds(128, 128)], brecv.at[0], bsem.at[0], up_y)
    arrived(arecv.at[1], asem.at[1])
    tsend[256:320, :] = tacc[256:320, :].astype(BF16)
    tsend[320:384, :] = (tacc[320:384, :] + arecv[1].astype(F32)).astype(BF16)
    send(tsend.at[pl.ds(256, 128)], brecv.at[1], bsem.at[1], down_y)
    iown[...] = image_dot(first)
    arrived(irecv, isem.at[0])
    iown[...] = iown[...] + irecv[...].astype(F32)
    zsend[...] = iown[...].astype(BF16)
    for k in (3, 2, 1, 0):
        to = device(xh, g, y, (z + first + k) % NZ, g)
        when = None if k else jnp.logical_not(source)
        send(zsend.at[pl.ds(k * N, N)], zrecv.at[z], zsem.at[z], to, when)
    arrived(brecv.at[0], bsem.at[0])
    arrived(brecv.at[1], bsem.at[1])
    total = tacc[384:512, :] + brecv[0].astype(F32) + brecv[1].astype(F32)
    tacc[384:512, :] = total
    xsend[...] = total.astype(BF16)
    for k in (0, 1):
        send(xsend.at[pl.ds(k * N, N)], xrecv.at[x], xsem.at[x], device(k, 1, y, z, core), x != 2 * k + 1)

    @pl.when(source)
    def _():
        acc = iown[0:N, :]
        for j in range(1, NZ):
            k = (z + j) % NZ
            arrived(zrecv.at[k], zsem.at[k])
            acc = acc + zrecv[k].astype(F32)
        out[0] = acc
        fsend[...] = acc.astype(BF16)

    send(fsend, frecv, fsem.at[0], beside, jnp.logical_and(source, g == 1))

    @pl.when(jnp.logical_and(g == 0, core == 1))
    def _():
        arrived(frecv, fsem.at[0])
        out[0] = frecv[...].astype(F32)

    @pl.when(g == 1)
    def _():
        acc = tacc[pl.ds(pl.multiple_of(384 + xh * N, N), N), :]
        for j in range(1, NX):
            k = (x + j) % NX
            arrived(xrecv.at[k], xsem.at[k])
            acc = acc + xrecv[k].astype(F32)
        out[0] = acc

    for entry in pending:
        if entry is None:
            continue
        c, when = entry
        if when is None:
            c.wait_send()
        else:
            pl.when(when)(c.wait_send)


def per_device(teacher_image, teacher_text, student_image, student_text, scales):
    shard, width = teacher_image.shape
    assert shard == N
    dma = pltpu.SemaphoreType.DMA
    vmem = pltpu.VMEM
    any_ = pl.BlockSpec(memory_space=pl.ANY)
    return pl.pallas_call(
        kernel,
        out_shape=jax.ShapeDtypeStruct((1, N, width), F32),
        in_specs=[any_] * 4 + [pl.BlockSpec(memory_space=pltpu.SMEM)],
        out_specs=pl.BlockSpec(memory_space=pltpu.VMEM),
        scratch_shapes=[
            vmem((2, ROWS, width), BF16),
            vmem((2, COLS, width), BF16),
            vmem((2, ROWS, COLS), F32),
            vmem((128, 128), F32),
            vmem((8, 128), F32),
            vmem((NZ * NC, 8, 128), F32),
            vmem((NX * NY, 8, 128), F32),
            vmem((2, ROWS, 128), F32),
            vmem((ROWS, COLS), BF16),
            vmem((COLS, ROWS), BF16),
            vmem((COLS, width), F32),
            vmem((384, width), BF16),
            vmem((2, N, width), BF16),
            vmem((2, 128, width), BF16),
            vmem((128, width), BF16),
            vmem((NX, N, width), BF16),
            vmem((256, width), BF16),
            vmem((256, width), F32),
            vmem((256, width), BF16),
            vmem((256, width), BF16),
            vmem((NZ, N, width), BF16),
            vmem((N, width), BF16),
            vmem((N, width), BF16),
            dma((4,)),
            dma((SENDS + 16,)),
            dma((2, NZ)),
            dma((2, 2 * NY)),
            dma((NZ * NC,)),
            dma((NX * NY,)),
            dma((2,)),
            dma((2,)),
            dma((NX,)),
            dma((1,)),
            dma((NZ,)),
            dma((1,)),
        ],
        compiler_params=pltpu.CompilerParams(
            collective_id=0, has_side_effects=True, vmem_limit_bytes=48 * 2**20
        ),
    )(teacher_image, teacher_text, student_image, student_text, scales)


def solution(mesh):
    assert mesh.shape["group"] == 2 and mesh.shape["batch"] == 2 * NY * NZ * NC
    return jax.shard_map(
        per_device,
        mesh=mesh,
        in_specs=(P("batch", None), P("batch", None), P("batch", None), P("batch", None), P()),
        out_specs=P("group", "batch", None),
        check_vma=False,
    )
```

time: 184 us -> 69.2 us (0.38)
  the two profiles are of different devices: /device:TPU:2 before, /device:TPU:33 now
where the time goes in v1:
time: 69.2 us; the launch traced here: 69 us
  Pallas kernels  64 us (92%)
  local copies, waits for them, and re-layouts  4.9 us (7%)
    pallas_call x1, Pallas kernels, per_device(): pl.pallas_call(kernel, out_shape=jax.ShapeDtypeStruct((1, N, width), F32)...  64 us
    unnamed x11, local copies, waits for them, and re-layouts  4.9 us

profile of v1, /device:TPU:33, one launch (start us, length us, event | category | flops | bytes accessed | tf_op | source)
XLA Modules:
  0.0 69.0 jit_solution(13020574221631480242)
XLA Ops:
  0.0 0.0 copy-start
  0.0 0.9 %copy-done = bf16[64,768]{1,0:T(8,128)(2,1)S(1)} copy-done((bf16[64,768]{1,0:T(8,128)(2,1)S(1)}, bf16[64,768]{1,0:T(8,128)(2,1)}, u32[]{:S(2)}) %copy-start) | copy-done | bytes 98328
  0.9 0.0 copy-start.1
  0.9 0.9 %copy-done.1 = bf16[64,768]{1,0:T(8,128)(2,1)S(1)} copy-done((bf16[64,768]{1,0:T(8,128)(2,1)S(1)}, bf16[64,768]{1,0:T(8,128)(2,1)}, u32[]{:S(2)}) %copy-start.1) | copy-done | bytes 98328
  1.8 0.0 copy-start.2
  1.8 0.9 %copy-done.2 = bf16[64,768]{1,0:T(8,128)(2,1)S(1)} copy-done((bf16[64,768]{1,0:T(8,128)(2,1)S(1)}, bf16[64,768]{1,0:T(8,128)(2,1)}, u32[]{:S(2)}) %copy-start.2) | copy-done | bytes 98328
  2.7 0.0 copy-start.3
  2.7 0.9 %copy-done.3 = bf16[64,768]{1,0:T(8,128)(2,1)S(1)} copy-done((bf16[64,768]{1,0:T(8,128)(2,1)S(1)}, bf16[64,768]{1,0:T(8,128)(2,1)}, u32[]{:S(2)}) %copy-start.3) | copy-done | bytes 98328
  3.6 0.0 copy-start.4
  3.6 0.7 copy-done.4
  4.2 64.0 %shard_map.55 = f32[1,64,768]{2,1,0:T(8,128)S(1)} custom-call(bf16[64,768]{1,0:T(8,128)(2,1)S(1)} %copy-done, bf16[64,768]{1,0:T(8,128)(2,1)S(1)} %copy-done.1, bf16[64,768]{1,0:T(8,128)(2,1)S(1)} %copy-done.2, bf16[64,768]{1,0:T(8,128)(2,1)S(1)} %copy-done.3, f32[2]{0:T(128)S(1)} %copy-done.4), custom_call_target="tpu_custom_call" | custom-call | tf_op jit(solution)/shard_map/pallas_call | solution.py:377
  68.3 0.7 copy.7
Async XLA Ops:
  0.0 0.9 %copy-start = (bf16[64,768]{1,0:T(8,128)(2,1)S(1)}, bf16[64,768]{1,0:T(8,128)(2,1)}, u32[]{:S(2)}) copy-start(bf16[64,768]{1,0:T(8,128)(2,1)} %ti.1) | copy-start | bytes 294916
  0.9 0.9 %copy-start.1 = (bf16[64,768]{1,0:T(8,128)(2,1)S(1)}, bf16[64,768]{1,0:T(8,128)(2,1)}, u32[]{:S(2)}) copy-start(bf16[64,768]{1,0:T(8,128)(2,1)} %tt.1) | copy-start | bytes 294916
  1.8 0.9 %copy-start.2 = (bf16[64,768]{1,0:T(8,128)(2,1)S(1)}, bf16[64,768]{1,0:T(8,128)(2,1)}, u32[]{:S(2)}) copy-start(bf16[64,768]{1,0:T(8,128)(2,1)} %si.1) | copy-start | bytes 294916
  2.7 0.9 %copy-start.3 = (bf16[64,768]{1,0:T(8,128)(2,1)S(1)}, bf16[64,768]{1,0:T(8,128)(2,1)}, u32[]{:S(2)}) copy-start(bf16[64,768]{1,0:T(8,128)(2,1)} %st.1) | copy-start | bytes 294916
  3.6 0.7 copy-start.4

commit v2 on v1

--- a/solution.py
+++ b/solution.py
@@ -22,8 +22,8 @@
 def kernel(
     ti, tt, si, st, scales, out,
     rows, cols, logits, rowst, stat, rstat, cstat, rcol, cpl, cplt,
-    tacc, tsend, arecv, brecv, xsend, xrecv, isend, iown, irecv, zsend, zrecv, fsend, frecv,
-    lsem, ssem, rsem, csem, rssem, cssem, asem, bsem, xsem, isem, zsem, fsem,
+    tacc, tsend, arecv, brecv, xsend, xrecv, isend, iown, irecv, zsend, zrecv, scale,
+    lsem, ssem, rsem, csem, rssem, cssem, asem, bsem, xsem, isem, zsem,
 ):
     width = ti.shape[1]
     b = lax.axis_index("batch")
@@ -58,6 +58,15 @@
         else:
             pl.when(when)(c.start)
 
+    def finish():
+        for entry in pending:
+            if entry is not None:
+                c, when = entry
+                if when is None:
+                    c.wait_send()
+                else:
+                    pl.when(when)(c.wait_send)
+
     def arrived(dst, sem):
         pltpu.make_async_remote_copy(
             src_ref=dst, dst_ref=dst, send_sem=ssem.at[SENDS - 1], recv_sem=sem, device_id=sibling, device_id_type=MESH
@@ -76,6 +85,7 @@
     locals_ = [
         pltpu.make_async_copy(tt, col_at(0, mine), lsem.at[0]),
         pltpu.make_async_copy(st, col_at(1, mine), lsem.at[1]),
+        pltpu.make_async_copy(scales, scale, lsem.at[4]),
     ]
     row_locals = [
         pltpu.make_async_copy(ti, row_at(0, z), lsem.at[2]),
@@ -193,7 +203,7 @@
         got_col(m1, col_slot(yy, 1 - xh))
 
     for m in (0, 1):
-        factor = scales[m]
+        factor = scale[m]
 
         @pl.loop(0, ROWS // 256)
         def _(i):
@@ -288,7 +298,7 @@
         cpl[block, :] = c.astype(BF16)
         cplt[:, block] = c.T.astype(BF16)
 
-    factor = scales[1]
+    factor = scale[1]
 
     def text_dot(ya, yb):
         a = jnp.concatenate([cplt[pl.ds(pl.multiple_of(k * 128, 128), 128), :] for k in (ya, yb)], axis=0)
@@ -299,55 +309,67 @@
         a = jnp.concatenate([cpl[pl.ds(pl.multiple_of(k * N, N), N), :] for k in parts], axis=0)
         return factor * jnp.dot(a, cols[1], preferred_element_type=F32)
 
+    def text_send(k, dst, sem, to):
+        send(tsend.at[pl.ds(k * N, N)], dst, sem, to)
+
     far = text_dot(y2, yu)
-    tacc[0:256, :] = far
     tsend[0:128, :] = far[0:128].astype(BF16)
-    send(tsend.at[pl.ds(0, N)], arecv.at[0], asem.at[0], up_y)
-    send(tsend.at[pl.ds(N, N)], arecv.at[1], asem.at[1], down_y)
+    text_send(0, arecv.at[0], asem.at[0], up_y)
+    text_send(1, arecv.at[1], asem.at[1], down_y)
+    tsend[192:256, :] = far[192:256].astype(BF16)
+    text_send(3, brecv.at[1], bsem.at[1], up_y)
+    tacc[128:192, :] = far[128:192]
     first = 4 * ((core + g) % 2)
     isend[...] = image_dot(4 - first).astype(BF16)
     send(isend, irecv, isem.at[0], sibling)
-    tacc[256:512, :] = text_dot(yd, y)
+    near = text_dot(yd, y)
+    tsend[256:320, :] = near[0:64].astype(BF16)
+    text_send(4, brecv.at[2], bsem.at[2], down_y)
+    tacc[320:512, :] = near[64:256]
+    iown[...] = image_dot(first)
+    arrived(irecv, isem.at[0])
+    mine_too = jnp.logical_or(g == 1, core == 1)
+    for k in (3, 2, 1, 0):
+        part = slice(k * N, (k + 1) * N)
+        summed = iown[part, :] + irecv[part, :].astype(F32)
+        if k == 0:
+            iown[part, :] = summed
+        zsend[part, :] = summed.astype(BF16)
+        to = device(xh, 0, y, (z + first + k) % NZ, g)
+        send(zsend.at[pl.ds(k * N, N)], zrecv.at[z], zsem.at[z], to, None if k else mine_too)
     arrived(arecv.at[0], asem.at[0])
     tsend[128:192, :] = (tacc[128:192, :] + arecv[0].astype(F32)).astype(BF16)
-    tsend[192:256, :] = tacc[192:256, :].astype(BF16)
-    send(tsend.at[pl.ds(128, 128)], brecv.at[0], bsem.at[0], up_y)
+    text_send(2, brecv.at[0], bsem.at[0], up_y)
     arrived(arecv.at[1], asem.at[1])
-    tsend[256:320, :] = tacc[256:320, :].astype(BF16)
     tsend[320:384, :] = (tacc[320:384, :] + arecv[1].astype(F32)).astype(BF16)
-    send(tsend.at[pl.ds(256, 128)], brecv.at[1], bsem.at[1], down_y)
-    iown[...] = image_dot(first)
-    arrived(irecv, isem.at[0])
-    iown[...] = iown[...] + irecv[...].astype(F32)
-    zsend[...] = iown[...].astype(BF16)
-    for k in (3, 2, 1, 0):
-        to = device(xh, g, y, (z + first + k) % NZ, g)
-        when = None if k else jnp.logical_not(source)
-        send(zsend.at[pl.ds(k * N, N)], zrecv.at[z], zsem.at[z], to, when)
-    arrived(brecv.at[0], bsem.at[0])
-    arrived(brecv.at[1], bsem.at[1])
-    total = tacc[384:512, :] + brecv[0].astype(F32) + brecv[1].astype(F32)
-    tacc[384:512, :] = total
-    xsend[...] = total.astype(BF16)
+    text_send(5, brecv.at[3], bsem.at[3], down_y)
+    for k in (1, 2, 0, 3):
+        arrived(brecv.at[k], bsem.at[k])
     for k in (0, 1):
+        part = slice(384 + k * N, 384 + (k + 1) * N)
+        total = tacc[part, :] + (brecv[k].astype(F32) + brecv[2 + k].astype(F32))
+        tacc[part, :] = total
+        xsend[k * N : (k + 1) * N, :] = total.astype(BF16)
         send(xsend.at[pl.ds(k * N, N)], xrecv.at[x], xsem.at[x], device(k, 1, y, z, core), x != 2 * k + 1)
 
-    @pl.when(source)
-    def _():
-        acc = iown[0:N, :]
-        for j in range(1, NZ):
-            k = (z + j) % NZ
-            arrived(zrecv.at[k], zsem.at[k])
-            acc = acc + zrecv[k].astype(F32)
-        out[0] = acc
-        fsend[...] = acc.astype(BF16)
-
-    send(fsend, frecv, fsem.at[0], beside, jnp.logical_and(source, g == 1))
+    def received(k):
+        arrived(zrecv.at[k], zsem.at[k])
+        return zrecv[k].astype(F32)
+
+    @pl.when(g == 0)
+    def _():
+        acc = received((z + 1) % NZ)
+        for j in (7, 2, 6, 3, 5, 4):
+            acc = acc + received((z + j) % NZ)
+        tacc[0:N, :] = acc
+
+    @pl.when(jnp.logical_and(g == 0, core == 0))
+    def _():
+        out[0] = tacc[0:N, :] + iown[0:N, :]
 
     @pl.when(jnp.logical_and(g == 0, core == 1))
     def _():
-        arrived(frecv, fsem.at[0])
-        out[0] = frecv[...].astype(F32)
+        out[0] = tacc[0:N, :] + received(z)
 
     @pl.when(g == 1)
     def _():
@@ -358,14 +380,7 @@
             acc = acc + xrecv[k].astype(F32)
         out[0] = acc
 
-    for entry in pending:
-        if entry is None:
-            continue
-        c, when = entry
-        if when is None:
-            c.wait_send()
-        else:
-            pl.when(when)(c.wait_send)
+    finish()
 
 
 def per_device(teacher_image, teacher_text, student_image, student_text, scales):
@@ -373,11 +388,11 @@
     assert shard == N
     dma = pltpu.SemaphoreType.DMA
     vmem = pltpu.VMEM
-    any_ = pl.BlockSpec(memory_space=pl.ANY)
+    any_ = pl.BlockSpec(memory_space=pltpu.HBM)
     return pl.pallas_call(
         kernel,
         out_shape=jax.ShapeDtypeStruct((1, N, width), F32),
-        in_specs=[any_] * 4 + [pl.BlockSpec(memory_space=pltpu.SMEM)],
+        in_specs=[any_] * 5,
         out_specs=pl.BlockSpec(memory_space=pltpu.VMEM),
         scratch_shapes=[
             vmem((2, ROWS, width), BF16),
@@ -393,7 +408,7 @@
             vmem((COLS, width), F32),
             vmem((384, width), BF16),
             vmem((2, N, width), BF16),
-            vmem((2, 128, width), BF16),
+            vmem((4, N, width), BF16),
             vmem((128, width), BF16),
             vmem((NX, N, width), BF16),
             vmem((256, width), BF16),
@@ -401,23 +416,21 @@
             vmem((256, width), BF16),
             vmem((256, width), BF16),
             vmem((NZ, N, width), BF16),
-            vmem((N, width), BF16),
-            vmem((N, width), BF16),
-            dma((4,)),
+            pltpu.SMEM((2,), F32),
+            dma((5,)),
             dma((SENDS + 16,)),
             dma((2, NZ)),
             dma((2, 2 * NY)),
             dma((NZ * NC,)),
             dma((NX * NY,)),
             dma((2,)),
-            dma((2,)),
+            dma((4,)),
             dma((NX,)),
             dma((1,)),
             dma((NZ,)),
-            dma((1,)),
         ],
         compiler_params=pltpu.CompilerParams(
-            collective_id=0, has_side_effects=True, vmem_limit_bytes=48 * 2**20
+            collective_id=0, has_side_effects=True, vmem_limit_bytes=62 * 2**20
         ),
     )(teacher_image, teacher_text, student_image, student_text, scales)
 

time: 69.2 us -> 61 us (0.88)
  the two profiles are of different devices: /device:TPU:33 before, /device:TPU:7 now
where the time goes in v2:
time: 61 us; the launch traced here: 60.9 us
  Pallas kernels  59.3 us (97%)
  local copies, waits for them, and re-layouts  1.62 us (3%)
    pallas_call x1, Pallas kernels, per_device(): pl.pallas_call(kernel, out_shape=jax.ShapeDtypeStruct((1, N, width), F32)...  59.3 us
    unnamed x1, local copies, waits for them, and re-layouts  1.62 us

profile of v2, /device:TPU:7, one launch (start us, length us, event | category | flops | bytes accessed | tf_op | source)
XLA Modules:
  0.0 60.9 jit_solution(13693573519557393424)
XLA Ops:
  0.0 59.3 %shard_map.55 = f32[1,64,768]{2,1,0:T(8,128)} custom-call(bf16[64,768]{1,0:T(8,128)(2,1)} %ti.1, bf16[64,768]{1,0:T(8,128)(2,1)} %tt.1, bf16[64,768]{1,0:T(8,128)(2,1)} %si.1, bf16[64,768]{1,0:T(8,128)(2,1)} %st.1, f32[2]{0:T(128)} %scales.1), custom_call_target="tpu_custom_call" | custom-call | tf_op jit(solution)/shard_map/pallas_call | solution.py:392
  59.3 1.6 %copy.7 = f32[1,64,768]{2,1,0:T(8,128)} copy(f32[1,64,768]{2,1,0:T(8,128)} %shard_map.55) | data formatting | bytes 393216

commit v3 on v2

--- a/solution.py
+++ b/solution.py
@@ -23,7 +23,7 @@
     ti, tt, si, st, scales, out,
     rows, cols, logits, rowst, stat, rstat, cstat, rcol, cpl, cplt,
     tacc, tsend, arecv, brecv, xsend, xrecv, isend, iown, irecv, zsend, zrecv, scale,
-    lsem, ssem, rsem, csem, rssem, cssem, asem, bsem, xsem, isem, zsem,
+    lsem, ssem, stsem, rsem, csem, rssem, cssem, asem, bsem, xsem, isem, zsem,
 ):
     width = ti.shape[1]
     b = lax.axis_index("batch")
@@ -59,6 +59,7 @@
             pl.when(when)(c.start)
 
     def finish():
+        assert len(pending) < SENDS
         for entry in pending:
             if entry is not None:
                 c, when = entry
@@ -126,10 +127,8 @@
         for c in row_locals:
             c.wait()
 
-    m1, m2 = g, 1 - g
-
-    def send_col(m, k, to, when=None):
-        send(col_at(m, k), col_at(m, k), csem.at[m, k], to, when)
+    def send_col(m, k, to):
+        send(col_at(m, k), col_at(m, k), csem.at[m, k], to)
 
     def send_row(m, k, to, when=None):
         send(row_at(m, k), row_at(m, k), rsem.at[m, k], to, when)
@@ -140,69 +139,86 @@
     def got_row(m, k):
         arrived(row_at(m, k), rsem.at[m, k])
 
-    zu, zd = (z + 1) % NZ, (z + NZ - 1) % NZ
-    send_col(m1, mine, across)
-    send_col(m1, mine, up_y)
-    send_col(m1, mine, down_y)
-    for m in (0, 1):
-        send_row(m, z, device(xh, g, y, zu, 0), source)
-        send_row(m, z, device(xh, g, y, zd, 1), source)
-    send_col(m2, mine, up_y)
-    send_col(m2, mine, down_y)
-    for m in (0, 1):
-        send_row(m, z, sibling, source)
-
-    def z_hop(d, models, onward):
-        k = (z - step * d + NZ) % NZ
-        for m in models:
-            got_row(m, k)
-            if onward == "all":
-                send_row(m, k, along)
-            send_row(m, k, sibling)
-        if onward == "own":
-            send_row(core, k, along)
-
-    def x_hop(yy):
-        k = col_slot(yy, 1 - xh)
-        got_col(m2, k)
-        send_col(m2, k, beside)
-
-    def y_slot(yy):
-        return col_slot(yy, xh)
-
-    z_hop(1, (0, 1), "all")
-    x_hop(y)
-    got_col(m1, y_slot(yd))
-    send_col(m1, y_slot(yd), up_y)
-    send_col(m1, y_slot(yd), across)
-    got_col(m1, y_slot(yu))
-    send_col(m1, y_slot(yu), across)
-    z_hop(2, (0, 1), "all")
-    got_col(m2, y_slot(yu))
-    send_col(m2, y_slot(yu), down_y)
-    got_col(m2, y_slot(yd))
-    x_hop(yd)
-    x_hop(yu)
-    z_hop(3, (0, 1), "own")
-    got_col(m1, y_slot(y2))
-    send_col(m1, y_slot(y2), across)
-    got_col(m2, y_slot(y2))
-    z_hop(4, (core,), None)
-    x_hop(y2)
-    for d in (1, 2, 3):
-        for m in (0, 1):
+    def z_from(d):
+        return (z - step * d + NZ) % NZ
+
+    def z_start(m, d):
+        send_row(m, z, device(xh, g, y, (z + d) % NZ, 0), source)
+        send_row(m, z, device(xh, g, y, (z + NZ - d) % NZ, 1), source)
+
+    def z_pass(m):
+        k = z_from(2)
+        got_row(m, k)
+        send_row(m, k, device(xh, g, y, (z + step + NZ) % NZ, core))
+        send_row(m, k, device(xh, g, y, (z + 2 * step + NZ) % NZ, core), core == m)
+        send_row(m, k, sibling)
+
+    def y_start(m):
+        send_col(m, mine, device(xh, g, y2, z, core))
+        send_col(m, mine, up_y)
+        send_col(m, mine, down_y)
+
+    def x_pass(m):
+        k = col_slot(y, 1 - xh)
+        got_col(m, k)
+        send_col(m, k, up_y)
+        send_col(m, k, down_y)
+
+    def y_pass(m):
+        k = col_slot(y2, xh)
+        got_col(m, k)
+        send_col(m, k, across)
+
+    def z_rest(m):
+        for d in (1, 3):
+            got_row(m, z_from(d))
+            send_row(m, z_from(d), sibling)
+        far = z_from(4)
+
+        @pl.when(core == m)
+        def _():
+            got_row(m, far)
+
+        send_row(m, far, sibling, core == m)
+
+    def complete(m):
+        for yy in (yu, yd):
+            got_col(m, col_slot(yy, xh))
+            got_col(m, col_slot(yy, 1 - xh))
+        got_col(m, col_slot(y2, 1 - xh))
+        for d in (1, 2, 3):
             got_row(m, (z + step * d + NZ) % NZ)
-    got_row(other, (z + 4) % NZ)
-
-    @pl.when(jnp.logical_not(source))
-    def _():
-        for m in (0, 1):
+
+        @pl.when(core != m)
+        def _():
+            got_row(m, (z + 4) % NZ)
+
+        @pl.when(jnp.logical_not(source))
+        def _():
             got_row(m, z)
 
-    for yy in (y, yd, yu, y2):
-        got_col(m1, col_slot(yy, 1 - xh))
-
-    for m in (0, 1):
+    send_col(0, mine, across)
+    z_start(0, 2)
+    y_start(0)
+    z_start(0, 1)
+    send_col(1, mine, across)
+    z_start(1, 2)
+    send_row(0, z, sibling, source)
+    x_pass(0)
+    y_start(1)
+    z_pass(0)
+    z_start(1, 1)
+    send_row(1, z, sibling, source)
+    y_pass(0)
+    x_pass(1)
+    z_pass(1)
+    y_pass(1)
+    z_rest(0)
+    complete(0)
+
+    lane = lax.broadcasted_iota(jnp.int32, (N, 128), 1)
+
+    def tile(m):
         factor = scale[m]
 
         @pl.loop(0, ROWS // 256)
@@ -212,9 +228,8 @@
                 rows[m, block, :], cols[m], (((1,), (1,)), ((), ())), preferred_element_type=F32
             )
 
-    lane = lax.broadcasted_iota(jnp.int32, (N, 128), 1)
-    rowst[...] = jnp.zeros_like(rowst)
-    for m in (0, 1):
+    def local_stats(m):
+        rowst[...] = jnp.zeros_like(rowst)
 
         def local(i, state):
             peak, total = state
@@ -222,7 +237,7 @@
             row_peak = jnp.max(l, axis=1, keepdims=True)
             row_lse = row_peak + jnp.log(jnp.sum(jnp.exp(l - row_peak), axis=1, keepdims=True))
             half = pl.ds(pl.multiple_of((i % 2) * N, N), N)
-            rowst[half, :] = jnp.where(lane == 4 * m + i // 2, row_lse, rowst[half, :])
+            rowst[half, :] = jnp.where(lane == i // 2, row_lse, rowst[half, :])
             now = jnp.maximum(peak, jnp.max(l, axis=0, keepdims=True))
             total = total * jnp.exp(peak - now) + jnp.sum(jnp.exp(l - now), axis=0, keepdims=True)
             return now, total
@@ -230,73 +245,79 @@
         start = (jnp.full((1, COLS), -3.0e38, F32), jnp.zeros((1, COLS), F32))
         peak, total = lax.fori_loop(0, ROWS // N, local, start)
         col_lse = peak + jnp.log(total)
-        for i in range(COLS // 128):
-            stat[4 * m + i : 4 * m + i + 1, :] = col_lse[:, 128 * i : 128 * (i + 1)]
-
-    cstat[col_me] = stat[...]
-    rstat[row_me] = rowst[...].T[:8, :]
-    sent = len(pending)
-
-    def stat_copy(kind, j):
-        if kind == 0:
-            q, to = row_peer(j)
-            return pltpu.make_async_remote_copy(
-                src_ref=rstat.at[row_me], dst_ref=rstat.at[row_me], send_sem=ssem.at[sent + j], recv_sem=rssem.at[row_me],
-                device_id=to, device_id_type=MESH,
-            ), q
-        q, to = col_peer(j)
-        return pltpu.make_async_remote_copy(
-            src_ref=cstat.at[col_me], dst_ref=cstat.at[col_me], send_sem=cssend(j), recv_sem=cssem.at[col_me],
-            device_id=to, device_id_type=MESH,
-        ), q
-
-    def cssend(j):
-        return ssem.at[SENDS + j]
-
-    @pl.loop(1, 16)
-    def _(j):
-        stat_copy(0, j)[0].start()
-        stat_copy(1, j)[0].start()
-
-    @pl.loop(1, 16)
-    def _(j):
-        q = row_peer(j)[0]
-        arrived(rstat.at[q], rssem.at[q])
-        q = col_peer(j)[0]
-        arrived(cstat.at[q], cssem.at[q])
-
-    @pl.loop(1, 16)
-    def _(j):
-        stat_copy(0, j)[0].wait_send()
-        stat_copy(1, j)[0].wait_send()
-
-    pending.extend([None] * 16)
+        parts = [col_lse[:, 128 * i : 128 * (i + 1)] for i in range(COLS // 128)]
+        cstat[m, col_me] = jnp.concatenate(parts + [jnp.zeros((8 - len(parts), 128), F32)], axis=0)
+        rstat[m, row_me] = rowst[...].T[:8, :]
+
+    def stat_copies(m, j):
+        return [
+            pltpu.make_async_remote_copy(
+                src_ref=ref.at[m, me], dst_ref=ref.at[m, me], send_sem=stsem.at[m, kind, j], recv_sem=sem.at[m, me],
+                device_id=peer(j)[1], device_id_type=MESH,
+            )
+            for kind, (ref, sem, me, peer) in enumerate(
+                ((rstat, rssem, row_me, row_peer), (cstat, cssem, col_me, col_peer))
+            )
+        ]
+
+    def stats_start(m):
+        @pl.loop(1, 16)
+        def _(j):
+            for c in stat_copies(m, j):
+                c.start()
 
     def joined(all_):
         peak = jnp.max(all_, axis=0)
         return peak + jnp.log(jnp.sum(jnp.exp(all_ - peak[None]), axis=0))
 
-    stat[...] = joined(cstat[...])
-    rowst[0:8, :] = joined(rstat[...])
-    turned = rowst[...].T
-    for m in (0, 1):
+    def stats_end(m):
+        @pl.loop(1, 16)
+        def _(j):
+            arrived(rstat.at[m, row_peer(j)[0]], rssem.at[m, row_peer(j)[0]])
+            arrived(cstat.at[m, col_peer(j)[0]], cssem.at[m, col_peer(j)[0]])
+
+        stat[...] = joined(cstat[m])
+        rowst[0:8, :] = joined(rstat[m])
+        turned = rowst[...].T
         for i in range(ROWS // 128):
-            rcol[m, 128 * i : 128 * (i + 1), :] = jnp.broadcast_to(turned[:, 4 * m + i : 4 * m + i + 1], (128, 128))
-    col_lse = [
-        jnp.concatenate([stat[4 * m + i : 4 * m + i + 1, :] for i in range(COLS // 128)], axis=1) for m in (0, 1)
-    ]
+            rcol[m, 128 * i : 128 * (i + 1), :] = jnp.broadcast_to(turned[:, i : i + 1], (128, 128))
+        return jnp.concatenate([stat[i : i + 1, :] for i in range(COLS // 128)], axis=1)
+
+    def chances(m, block, col_lse):
+        l = logits[m, block, :]
+        r = jnp.concatenate([rcol[m, block, :]] * (COLS // 128), axis=1)
+        return jnp.exp(l - r) + jnp.exp(l - col_lse)
+
+    tile(0)
+    local_stats(0)
+    stats_start(0)
+    z_rest(1)
+    complete(1)
+    tile(1)
+    local_stats(1)
+    stats_start(1)
+    teacher_lse = stats_end(0)
 
     @pl.loop(0, ROWS // 128)
     def _(i):
         block = pl.ds(pl.multiple_of(i * 128, 128), 128)
-        terms = []
-        for m in (0, 1):
-            l = logits[m, block, :]
-            r = jnp.concatenate([rcol[m, block, :]] * (COLS // 128), axis=1)
-            terms.append((jnp.exp(l - r), jnp.exp(l - col_lse[m])))
-        c = 0.5 * ((terms[1][0] - terms[0][0]) + (terms[1][1] - terms[0][1]))
+        logits[0, block, :] = chances(0, block, teacher_lse)
+
+    student_lse = stats_end(1)
+
+    @pl.loop(0, ROWS // 128)
+    def _(i):
+        block = pl.ds(pl.multiple_of(i * 128, 128), 128)
+        c = 0.5 * (chances(1, block, student_lse) - logits[0, block, :])
         cpl[block, :] = c.astype(BF16)
         cplt[:, block] = c.T.astype(BF16)
+
+    for m in (0, 1):
+
+        @pl.loop(1, 16)
+        def _(j):
+            for c in stat_copies(m, j):
+                c.wait_send()
 
     factor = scale[1]
 
@@ -400,8 +421,8 @@
             vmem((2, ROWS, COLS), F32),
             vmem((128, 128), F32),
             vmem((8, 128), F32),
-            vmem((NZ * NC, 8, 128), F32),
-            vmem((NX * NY, 8, 128), F32),
+            vmem((2, NZ * NC, 8, 128), F32),
+            vmem((2, NX * NY, 8, 128), F32),
             vmem((2, ROWS, 128), F32),
             vmem((ROWS, COLS), BF16),
             vmem((COLS, ROWS), BF16),
@@ -418,11 +439,12 @@
             vmem((NZ, N, width), BF16),
             pltpu.SMEM((2,), F32),
             dma((5,)),
-            dma((SENDS + 16,)),
+            dma((SENDS,)),
+            dma((2, 2, 16)),
             dma((2, NZ)),
             dma((2, 2 * NY)),
-            dma((NZ * NC,)),
-            dma((NX * NY,)),
+            dma((2, NZ * NC)),
+            dma((2, NX * NY)),
             dma((2,)),
             dma((4,)),
             dma((NX,)),

time: 61 us -> 57.5 us (0.943)
  the two profiles are of different devices: /device:TPU:7 before, /device:TPU:2 now
where the time goes in v3:
time: 57.5 us; the launch traced here: 56.5 us
  Pallas kernels  54.9 us (95%)
  local copies, waits for them, and re-layouts  1.62 us (3%)
    pallas_call x1, Pallas kernels, per_device(): pl.pallas_call(kernel, out_shape=jax.ShapeDtypeStruct((1, N, width), F32)...  54.9 us
    unnamed x1, local copies, waits for them, and re-layouts  1.62 us

profile of v3, /device:TPU:2, one launch (start us, length us, event | category | flops | bytes accessed | tf_op | source)
XLA Modules:
  0.0 56.5 jit_solution(9078859773088341944)
XLA Ops:
  0.0 54.9 %shard_map.55 = f32[1,64,768]{2,1,0:T(8,128)} custom-call(bf16[64,768]{1,0:T(8,128)(2,1)} %ti.1, bf16[64,768]{1,0:T(8,128)(2,1)} %tt.1, bf16[64,768]{1,0:T(8,128)(2,1)} %si.1, bf16[64,768]{1,0:T(8,128)(2,1)} %st.1, f32[2]{0:T(128)} %scales.1), custom_call_target="tpu_custom_call" | custom-call | tf_op jit(solution)/shard_map/pallas_call | solution.py:413
  54.9 1.6 %copy.7 = f32[1,64,768]{2,1,0:T(8,128)} copy(f32[1,64,768]{2,1,0:T(8,128)} %shard_map.55) | data formatting | bytes 393216

commit v4 on v3

--- a/solution.py
+++ b/solution.py
@@ -1,3 +1,5 @@
+import functools
+
 import jax
 import jax.numpy as jnp
 from jax import lax
@@ -13,6 +15,15 @@
 ROWS = NZ * N
 COLS = NY * 2 * N
 SENDS = 80
+FAR_FIRST = (8, 9, 7, 6, 10, 5, 11, 4, 12, 3, 13, 2, 14, 1, 15)
+
+
+def mod(a, n):
+    return lax.rem(a, jnp.int32(n))
+
+
+def div(a, n):
+    return lax.div(a, jnp.int32(n))
 
 
 def device(x_hi, x_lo, y, z, core):
@@ -21,25 +32,24 @@
 
 def kernel(
     ti, tt, si, st, scales, out,
-    rows, cols, logits, rowst, stat, rstat, cstat, rcol, cpl, cplt,
+    rows, cols, logits, stat, rstat, cstat, rcol, cpl, cplt,
     tacc, tsend, arecv, brecv, xsend, xrecv, isend, iown, irecv, zsend, zrecv, scale,
     lsem, ssem, stsem, rsem, csem, rssem, cssem, asem, bsem, xsem, isem, zsem,
 ):
     width = ti.shape[1]
     b = lax.axis_index("batch")
     g = lax.axis_index("group")
-    core, y, z, xh = b % NC, (b // NC) % NY, (b // (NC * NY)) % NZ, b // (NC * NY * NZ)
+    core, y, z, xh = mod(b, NC), mod(div(b, NC), NY), mod(div(b, NC * NY), NZ), div(b, NC * NY * NZ)
     x = 2 * xh + g
     other = 1 - core
     step = 1 - 2 * core
-    yu, yd, y2 = (y + 1) % NY, (y + 3) % NY, (y + 2) % NY
+    yu, yd, y2 = mod(y + 1, NY), mod(y + 3, NY), mod(y + 2, NY)
     source = core == g
 
     sibling = device(xh, g, y, z, other)
     up_y, down_y = device(xh, g, yu, z, core), device(xh, g, yd, z, core)
     across = device(1 - xh, 1 - g, y, z, core)
     beside = device(xh, 1 - g, y, z, core)
-    along = device(xh, g, y, (z + step + NZ) % NZ, core)
 
     pending = []
 
@@ -81,6 +91,24 @@
 
     def col_at(m, k):
         return cols.at[m, pl.ds(pl.multiple_of(k * N, N), N)]
+
+    row_me, col_me = z * NC + core, x * NY + y
+
+    def row_peer(j):
+        q = mod(row_me + j, NZ * NC)
+        return q, device(xh, g, y, div(q, NC), mod(q, NC))
+
+    def col_peer(j):
+        q = mod(col_me + j, NX * NY)
+        qx = div(q, NY)
+        return q, device(div(qx, 2), mod(qx, 2), mod(q, NY), z, core)
+
+    barrier = pltpu.get_barrier_semaphore()
+
+    @pl.loop(1, 16)
+    def _(j):
+        pl.semaphore_signal(barrier, inc=1, device_id=row_peer(j)[1], device_id_type=MESH)
+        pl.semaphore_signal(barrier, inc=1, device_id=col_peer(j)[1], device_id_type=MESH)
 
     mine = col_slot(y, xh)
     locals_ = [
@@ -100,38 +128,14 @@
         for c in row_locals:
             c.start()
 
-    row_me, col_me = z * NC + core, x * NY + y
-
-    def row_peer(j):
-        q = (row_me + j) % (NZ * NC)
-        return q, device(xh, g, y, q // NC, q % NC)
-
-    def col_peer(j):
-        q = (col_me + j) % (NX * NY)
-        qx = q // NY
-        return q, device(qx // 2, qx % 2, q % NY, z, core)
-
-    barrier = pltpu.get_barrier_semaphore()
-
-    @pl.loop(1, 16)
-    def _(j):
-        pl.semaphore_signal(barrier, inc=1, device_id=row_peer(j)[1], device_id_type=MESH)
-        pl.semaphore_signal(barrier, inc=1, device_id=col_peer(j)[1], device_id_type=MESH)
-
     pl.semaphore_wait(barrier, 30)
-    for c in locals_:
-        c.wait()
-
-    @pl.when(source)
-    def _():
-        for c in row_locals:
-            c.wait()
-
     def send_col(m, k, to):
-        send(col_at(m, k), col_at(m, k), csem.at[m, k], to)
+        src = (tt, st)[m] if k is mine else col_at(m, k)
+        send(src, col_at(m, k), csem.at[m, k], to)
 
     def send_row(m, k, to, when=None):
-        send(row_at(m, k), row_at(m, k), rsem.at[m, k], to, when)
+        src = (ti, si)[m] if k is z else row_at(m, k)
+        send(src, row_at(m, k), rsem.at[m, k], to, when)
 
     def got_col(m, k):
         arrived(col_at(m, k), csem.at[m, k])
@@ -140,17 +144,22 @@
         arrived(row_at(m, k), rsem.at[m, k])
 
     def z_from(d):
-        return (z - step * d + NZ) % NZ
+        return mod(z - step * d + NZ, NZ)
 
     def z_start(m, d):
-        send_row(m, z, device(xh, g, y, (z + d) % NZ, 0), source)
-        send_row(m, z, device(xh, g, y, (z + NZ - d) % NZ, 1), source)
+        send_row(m, z, device(xh, g, y, mod(z + d, NZ), 0), source)
+        send_row(m, z, device(xh, g, y, mod(z + NZ - d, NZ), 1), source)
+
+    def z_own(m):
+        z_start(m, 2)
+        z_start(m, 1)
+        send_row(m, z, sibling, source)
 
     def z_pass(m):
         k = z_from(2)
         got_row(m, k)
-        send_row(m, k, device(xh, g, y, (z + step + NZ) % NZ, core))
-        send_row(m, k, device(xh, g, y, (z + 2 * step + NZ) % NZ, core), core == m)
+        send_row(m, k, device(xh, g, y, mod(z + 2 * step + NZ, NZ), core), core == m)
+        send_row(m, k, device(xh, g, y, mod(z + step + NZ, NZ), core))
         send_row(m, k, sibling)
 
     def y_start(m):
@@ -170,9 +179,8 @@
         send_col(m, k, across)
 
     def z_rest(m):
-        for d in (1, 3):
-            got_row(m, z_from(d))
-            send_row(m, z_from(d), sibling)
+        got_row(m, z_from(1))
+        send_row(m, z_from(1), sibling)
         far = z_from(4)
 
         @pl.when(core == m)
@@ -180,6 +188,8 @@
             got_row(m, far)
 
         send_row(m, far, sibling, core == m)
+        got_row(m, z_from(3))
+        send_row(m, z_from(3), sibling)
 
     def complete(m):
         for yy in (yu, yd):
@@ -187,11 +197,11 @@
             got_col(m, col_slot(yy, 1 - xh))
         got_col(m, col_slot(y2, 1 - xh))
         for d in (1, 2, 3):
-            got_row(m, (z + step * d + NZ) % NZ)
+            got_row(m, mod(z + step * d + NZ, NZ))
 
         @pl.when(core != m)
         def _():
-            got_row(m, (z + 4) % NZ)
+            got_row(m, mod(z + 4, NZ))
 
         @pl.when(jnp.logical_not(source))
         def _():
@@ -201,22 +211,27 @@
     z_start(0, 2)
     y_start(0)
     z_start(0, 1)
+    send_row(0, z, sibling, source)
+    z_start(1, 2)
     send_col(1, mine, across)
-    z_start(1, 2)
-    send_row(0, z, sibling, source)
-    x_pass(0)
     y_start(1)
-    z_pass(0)
     z_start(1, 1)
     send_row(1, z, sibling, source)
+    x_pass(0)
+    z_pass(0)
     y_pass(0)
     x_pass(1)
     z_pass(1)
     y_pass(1)
     z_rest(0)
     complete(0)
-
-    lane = lax.broadcasted_iota(jnp.int32, (N, 128), 1)
+    for c in locals_:
+        c.wait()
+
+    @pl.when(source)
+    def _():
+        for c in row_locals:
+            c.wait()
 
     def tile(m):
         factor = scale[m]
@@ -229,25 +244,27 @@
             )
 
     def local_stats(m):
-        rowst[...] = jnp.zeros_like(rowst)
-
-        def local(i, state):
-            peak, total = state
-            l = logits[m, pl.ds(pl.multiple_of(i * N, N), N), :]
-            row_peak = jnp.max(l, axis=1, keepdims=True)
-            row_lse = row_peak + jnp.log(jnp.sum(jnp.exp(l - row_peak), axis=1, keepdims=True))
-            half = pl.ds(pl.multiple_of((i % 2) * N, N), N)
-            rowst[half, :] = jnp.where(lane == i // 2, row_lse, rowst[half, :])
-            now = jnp.maximum(peak, jnp.max(l, axis=0, keepdims=True))
-            total = total * jnp.exp(peak - now) + jnp.sum(jnp.exp(l - now), axis=0, keepdims=True)
-            return now, total
-
-        start = (jnp.full((1, COLS), -3.0e38, F32), jnp.zeros((1, COLS), F32))
-        peak, total = lax.fori_loop(0, ROWS // N, local, start)
-        col_lse = peak + jnp.log(total)
+        peak, total = jnp.full((8, COLS), -3.0e38, F32), jnp.zeros((8, COLS), F32)
+        row_lse = []
+        for i in range(ROWS // 128):
+            l = logits[m, 128 * i : 128 * (i + 1), :]
+            parts = [l[:, 128 * k : 128 * (k + 1)] for k in range(COLS // 128)]
+            lane_peak = functools.reduce(jnp.maximum, parts)
+            lane_total = functools.reduce(jnp.add, [jnp.exp(p - lane_peak) for p in parts])
+            lane_peak, lane_total = lane_peak.T, lane_total.T
+            row_peak = jnp.max(lane_peak, axis=0, keepdims=True)
+            row_total = jnp.sum(lane_total * jnp.exp(lane_peak - row_peak), axis=0, keepdims=True)
+            row_lse.append(row_peak + jnp.log(row_total))
+            l = l.reshape(16, 8, COLS)
+            now = jnp.maximum(peak, jnp.max(l, axis=0))
+            total = total * jnp.exp(peak - now) + jnp.sum(jnp.exp(l - now[None]), axis=0)
+            peak = now
+        col_peak = jnp.max(peak, axis=0, keepdims=True)
+        col_lse = col_peak + jnp.log(jnp.sum(total * jnp.exp(peak - col_peak), axis=0, keepdims=True))
         parts = [col_lse[:, 128 * i : 128 * (i + 1)] for i in range(COLS // 128)]
-        cstat[m, col_me] = jnp.concatenate(parts + [jnp.zeros((8 - len(parts), 128), F32)], axis=0)
-        rstat[m, row_me] = rowst[...].T[:8, :]
+        rest = [jnp.zeros((4, 128), F32)]
+        cstat[m, col_me] = jnp.concatenate(parts + rest, axis=0)
+        rstat[m, row_me] = jnp.concatenate(row_lse + rest, axis=0)
 
     def stat_copies(m, j):
         return [
@@ -261,8 +278,7 @@
         ]
 
     def stats_start(m):
-        @pl.loop(1, 16)
-        def _(j):
+        for j in FAR_FIRST:
             for c in stat_copies(m, j):
                 c.start()
 
@@ -277,8 +293,7 @@
             arrived(cstat.at[m, col_peer(j)[0]], cssem.at[m, col_peer(j)[0]])
 
         stat[...] = joined(cstat[m])
-        rowst[0:8, :] = joined(rstat[m])
-        turned = rowst[...].T
+        turned = jnp.concatenate([joined(rstat[m]), jnp.zeros((120, 128), F32)], axis=0).T
         for i in range(ROWS // 128):
             rcol[m, 128 * i : 128 * (i + 1), :] = jnp.broadcast_to(turned[:, i : i + 1], (128, 128))
         return jnp.concatenate([stat[i : i + 1, :] for i in range(COLS // 128)], axis=1)
@@ -289,9 +304,9 @@
         return jnp.exp(l - r) + jnp.exp(l - col_lse)
 
     tile(0)
+    z_rest(1)
     local_stats(0)
     stats_start(0)
-    z_rest(1)
     complete(1)
     tile(1)
     local_stats(1)
@@ -326,7 +341,7 @@
         return factor * jnp.dot(a, rows[1], preferred_element_type=F32)
 
     def image_dot(first):
-        parts = [(z + first + k) % NZ for k in range(4)]
+        parts = [mod(z + first + k, NZ) for k in range(4)]
         a = jnp.concatenate([cpl[pl.ds(pl.multiple_of(k * N, N), N), :] for k in parts], axis=0)
         return factor * jnp.dot(a, cols[1], preferred_element_type=F32)
 
@@ -340,7 +355,7 @@
     tsend[192:256, :] = far[192:256].astype(BF16)
     text_send(3, brecv.at[1], bsem.at[1], up_y)
     tacc[128:192, :] = far[128:192]
-    first = 4 * ((core + g) % 2)
+    first = 4 * mod(core + g, 2)
     isend[...] = image_dot(4 - first).astype(BF16)
     send(isend, irecv, isem.at[0], sibling)
     near = text_dot(yd, y)
@@ -356,7 +371,7 @@
         if k == 0:
             iown[part, :] = summed
         zsend[part, :] = summed.astype(BF16)
-        to = device(xh, 0, y, (z + first + k) % NZ, g)
+        to = device(xh, 0, y, mod(z + first + k, NZ), g)
         send(zsend.at[pl.ds(k * N, N)], zrecv.at[z], zsem.at[z], to, None if k else mine_too)
     arrived(arecv.at[0], asem.at[0])
     tsend[128:192, :] = (tacc[128:192, :] + arecv[0].astype(F32)).astype(BF16)
@@ -379,9 +394,9 @@
 
     @pl.when(g == 0)
     def _():
-        acc = received((z + 1) % NZ)
+        acc = received(mod(z + 1, NZ))
         for j in (7, 2, 6, 3, 5, 4):
-            acc = acc + received((z + j) % NZ)
+            acc = acc + received(mod(z + j, NZ))
         tacc[0:N, :] = acc
 
     @pl.when(jnp.logical_and(g == 0, core == 0))
@@ -396,7 +411,7 @@
     def _():
         acc = tacc[pl.ds(pl.multiple_of(384 + xh * N, N), N), :]
         for j in range(1, NX):
-            k = (x + j) % NX
+            k = mod(x + j, NX)
             arrived(xrecv.at[k], xsem.at[k])
             acc = acc + xrecv[k].astype(F32)
         out[0] = acc
@@ -419,7 +434,6 @@
             vmem((2, ROWS, width), BF16),
             vmem((2, COLS, width), BF16),
             vmem((2, ROWS, COLS), F32),
-            vmem((128, 128), F32),
             vmem((8, 128), F32),
             vmem((2, NZ * NC, 8, 128), F32),
             vmem((2, NX * NY, 8, 128), F32),

time: 57.5 us -> 53.1 us (0.923)
  Pallas kernels: 54.9 us -> 50.8 us
    pallas_call x1, Pallas kernels: 54.9 us -> 50.8 us  [per_device(): pl.pallas_call(kernel, out_shape=jax.ShapeDtypeStruct((1, N, width), F32)...]
where the time goes in v4:
time: 53.1 us; the launch traced here: 52.4 us
  Pallas kernels  50.8 us (96%)
  local copies, waits for them, and re-layouts  1.62 us (3%)
    pallas_call x1, Pallas kernels, per_device(): pl.pallas_call(kernel, out_shape=jax.ShapeDtypeStruct((1, N, width), F32)...  50.8 us
    unnamed x1, local copies, waits for them, and re-layouts  1.62 us

profile of v4, /device:TPU:2, one launch (start us, length us, event | category | flops | bytes accessed | tf_op | source)
XLA Modules:
  0.0 52.4 jit_solution(16508579038908112681)
XLA Ops:
  0.0 50.8 %shard_map.55 = f32[1,64,768]{2,1,0:T(8,128)} custom-call(bf16[64,768]{1,0:T(8,128)(2,1)} %ti.1, bf16[64,768]{1,0:T(8,128)(2,1)} %tt.1, bf16[64,768]{1,0:T(8,128)(2,1)} %si.1, bf16[64,768]{1,0:T(8,128)(2,1)} %st.1, f32[2]{0:T(128)} %scales.1), custom_call_target="tpu_custom_call" | custom-call | tf_op jit(solution)/shard_map/pallas_call | solution.py:428
  50.8 1.6 %copy.7 = f32[1,64,768]{2,1,0:T(8,128)} copy(f32[1,64,768]{2,1,0:T(8,128)} %shard_map.55) | data formatting | bytes 393216

commit v5 on v4

--- a/solution.py
+++ b/solution.py
@@ -33,8 +33,8 @@
 def kernel(
     ti, tt, si, st, scales, out,
     rows, cols, logits, stat, rstat, cstat, rcol, cpl, cplt,
-    tacc, tsend, arecv, brecv, xsend, xrecv, isend, iown, irecv, zsend, zrecv, scale,
-    lsem, ssem, stsem, rsem, csem, rssem, cssem, asem, bsem, xsem, isem, zsem,
+    tacc, tsend, arecv, brecv, xsend, xrecv, isend, iown, irecv, zsend, zrecv, crecv, scale,
+    lsem, ssem, stsem, rsem, csem, rssem, cssem, asem, bsem, xsem, isem, zsem, tosem,
 ):
     width = ti.shape[1]
     b = lax.axis_index("batch")
@@ -105,10 +105,10 @@
 
     barrier = pltpu.get_barrier_semaphore()
 
-    @pl.loop(1, 16)
-    def _(j):
-        pl.semaphore_signal(barrier, inc=1, device_id=row_peer(j)[1], device_id_type=MESH)
-        pl.semaphore_signal(barrier, inc=1, device_id=col_peer(j)[1], device_id_type=MESH)
+    near = [sibling, up_y, down_y, device(xh, g, y2, z, core), across, beside]
+    near += [device(xh, g, y, mod(z + d, NZ), c) for d in (1, 7, 2, 6) for c in (0, 1)]
+    for to in near:
+        pl.semaphore_signal(barrier, inc=1, device_id=to, device_id_type=MESH)
 
     mine = col_slot(y, xh)
     locals_ = [
@@ -128,7 +128,7 @@
         for c in row_locals:
             c.start()
 
-    pl.semaphore_wait(barrier, 30)
+    pl.semaphore_wait(barrier, len(near))
     def send_col(m, k, to):
         src = (tt, st)[m] if k is mine else col_at(m, k)
         send(src, col_at(m, k), csem.at[m, k], to)
@@ -358,27 +358,44 @@
     first = 4 * mod(core + g, 2)
     isend[...] = image_dot(4 - first).astype(BF16)
     send(isend, irecv, isem.at[0], sibling)
-    near = text_dot(yd, y)
-    tsend[256:320, :] = near[0:64].astype(BF16)
+    close = text_dot(yd, y)
+    tsend[256:320, :] = close[0:64].astype(BF16)
     text_send(4, brecv.at[2], bsem.at[2], down_y)
-    tacc[320:512, :] = near[64:256]
+    tacc[320:512, :] = close[64:256]
     iown[...] = image_dot(first)
     arrived(irecv, isem.at[0])
     mine_too = jnp.logical_or(g == 1, core == 1)
-    for k in (3, 2, 1, 0):
-        part = slice(k * N, (k + 1) * N)
-        summed = iown[part, :] + irecv[part, :].astype(F32)
-        if k == 0:
-            iown[part, :] = summed
-        zsend[part, :] = summed.astype(BF16)
+    down = div(first, 4)
+    toward = device(xh, g, y, mod(z + 1 + 6 * down, NZ), core)
+
+    def image_part(k):
+        return pl.ds(pl.multiple_of(k * N, N), N)
+
+    def image_sum(k):
+        summed = iown[image_part(k), :] + irecv[image_part(k), :].astype(F32)
+        iown[image_part(k), :] = summed
+        zsend[image_part(k), :] = summed.astype(BF16)
+
+    def image_send(k, when=None):
         to = device(xh, 0, y, mod(z + first + k, NZ), g)
-        send(zsend.at[pl.ds(k * N, N)], zrecv.at[z], zsem.at[z], to, None if k else mine_too)
+        send(zsend.at[image_part(k)], zrecv.at[z], zsem.at[z], to, when)
+
+    image_sum(3 - 2 * down)
+    send(zsend.at[image_part(3 - 2 * down)], crecv, tosem.at[0], toward)
+    image_sum(0)
+    image_send(0, mine_too)
+    image_sum(1 + 2 * down)
+    image_send(1 + 2 * down)
+    iown[image_part(2), :] = iown[image_part(2), :] + irecv[image_part(2), :].astype(F32)
     arrived(arecv.at[0], asem.at[0])
     tsend[128:192, :] = (tacc[128:192, :] + arecv[0].astype(F32)).astype(BF16)
     text_send(2, brecv.at[0], bsem.at[0], up_y)
     arrived(arecv.at[1], asem.at[1])
     tsend[320:384, :] = (tacc[320:384, :] + arecv[1].astype(F32)).astype(BF16)
     text_send(5, brecv.at[3], bsem.at[3], down_y)
+    arrived(crecv, tosem.at[0])
+    zsend[image_part(2), :] = (iown[image_part(2), :] + crecv[...].astype(F32)).astype(BF16)
+    image_send(2)
     for k in (1, 2, 0, 3):
         arrived(brecv.at[k], bsem.at[k])
     for k in (0, 1):
@@ -395,7 +412,7 @@
     @pl.when(g == 0)
     def _():
         acc = received(mod(z + 1, NZ))
-        for j in (7, 2, 6, 3, 5, 4):
+        for j in (7, 4, 2, 6):
             acc = acc + received(mod(z + j, NZ))
         tacc[0:N, :] = acc
 
@@ -424,6 +441,10 @@
     assert shard == N
     dma = pltpu.SemaphoreType.DMA
     vmem = pltpu.VMEM
+    teacher_image, teacher_text, student_image, student_text, scales = [
+        pltpu.with_memory_space_constraint(a, pltpu.HBM)
+        for a in (teacher_image, teacher_text, student_image, student_text, scales)
+    ]
     any_ = pl.BlockSpec(memory_space=pltpu.HBM)
     return pl.pallas_call(
         kernel,
@@ -451,6 +472,7 @@
             vmem((256, width), BF16),
             vmem((256, width), BF16),
             vmem((NZ, N, width), BF16),
+            vmem((N, width), BF16),
             pltpu.SMEM((2,), F32),
             dma((5,)),
             dma((SENDS,)),
@@ -464,9 +486,10 @@
             dma((NX,)),
             dma((1,)),
             dma((NZ,)),
+            dma((1,)),
         ],
         compiler_params=pltpu.CompilerParams(
-            collective_id=0, has_side_effects=True, vmem_limit_bytes=62 * 2**20
+            collective_id=0, has_side_effects=True, vmem_limit_bytes=48 * 2**20
         ),
     )(teacher_image, teacher_text, student_image, student_text, scales)
 

time: 53.1 us -> 49.5 us (0.932); the launches traced: 52.4 us -> 49.5 us
  Pallas kernels: 50.8 us -> 48.8 us
  local copies, waits for them, and re-layouts: 1.62 us -> 0.68 us
    pallas_call x1, Pallas kernels: 50.8 us -> 48.8 us  [per_device(): pl.pallas_call(kernel, out_shape=jax.ShapeDtypeStruct((1, N, width), F32)...]
    unnamed x1, local copies, waits for them, and re-layouts: 1.62 us -> 0.68 us
where the time goes in v5:
time: 49.5 us
  Pallas kernels  48.8 us (99%)
  local copies, waits for them, and re-layouts  0.68 us (1%)
    pallas_call x1, Pallas kernels, per_device(): pl.pallas_call(kernel, out_shape=jax.ShapeDtypeStruct((1, N, width), F32)...  48.8 us

profile of v5, /device:TPU:2, one launch (start us, length us, event | category | flops | bytes accessed | tf_op | source)
XLA Modules:
  0.0 49.5 jit_solution(3196953052961675151)
XLA Ops:
  0.0 48.8 %shard_map.55 = f32[1,64,768]{2,1,0:T(8,128)S(1)} custom-call(bf16[64,768]{1,0:T(8,128)(2,1)} %ti.1, bf16[64,768]{1,0:T(8,128)(2,1)} %tt.1, bf16[64,768]{1,0:T(8,128)(2,1)} %si.1, bf16[64,768]{1,0:T(8,128)(2,1)} %st.1, f32[2]{0:T(128)} %scales.1), custom_call_target="tpu_custom_call" | custom-call | tf_op jit(solution)/shard_map/pallas_call | solution.py:449
  48.8 0.7 %copy.7 = f32[1,64,768]{2,1,0:T(8,128)} copy(f32[1,64,768]{2,1,0:T(8,128)S(1)} %shard_map.55) | data formatting | bytes 393216

commit v6 on v5

--- a/solution.py
+++ b/solution.py
@@ -36,7 +36,6 @@
     tacc, tsend, arecv, brecv, xsend, xrecv, isend, iown, irecv, zsend, zrecv, crecv, scale,
     lsem, ssem, stsem, rsem, csem, rssem, cssem, asem, bsem, xsem, isem, zsem, tosem,
 ):
-    width = ti.shape[1]
     b = lax.axis_index("batch")
     g = lax.axis_index("group")
     core, y, z, xh = mod(b, NC), mod(div(b, NC), NY), mod(div(b, NC * NY), NZ), div(b, NC * NY * NZ)
@@ -212,9 +211,9 @@
     y_start(0)
     z_start(0, 1)
     send_row(0, z, sibling, source)
-    z_start(1, 2)
     send_col(1, mine, across)
     y_start(1)
+    z_start(1, 2)
     z_start(1, 1)
     send_row(1, z, sibling, source)
     x_pass(0)
@@ -236,12 +235,9 @@
     def tile(m):
         factor = scale[m]
 
-        @pl.loop(0, ROWS // 256)
-        def _(i):
-            block = pl.ds(pl.multiple_of(i * 256, 256), 256)
-            logits[m, block, :] = factor * lax.dot_general(
-                rows[m, block, :], cols[m], (((1,), (1,)), ((), ())), preferred_element_type=F32
-            )
+        logits[m] = factor * lax.dot_general(
+            rows[m], cols[m], (((1,), (1,)), ((), ())), preferred_element_type=F32
+        )
 
     def local_stats(m):
         peak, total = jnp.full((8, COLS), -3.0e38, F32), jnp.zeros((8, COLS), F32)

time: 49.5 us -> 49.3 us (level)
  Pallas kernels: 48.8 us -> 48.3 us
where the time goes in v6:
time: 49.3 us; the launch traced here: 49 us
  Pallas kernels  48.3 us (98%)
  local copies, waits for them, and re-layouts  0.68 us (1%)
    pallas_call x1, Pallas kernels, per_device(): pl.pallas_call(kernel, out_shape=jax.ShapeDtypeStruct((1, N, width), F32)...  48.3 us

profile of v6, /device:TPU:2, one launch (start us, length us, event | category | flops | bytes accessed | tf_op | source)
XLA Modules:
  0.0 49.0 jit_solution(10221803037230208633)
XLA Ops:
  0.0 48.3 %shard_map.55 = f32[1,64,768]{2,1,0:T(8,128)S(1)} custom-call(bf16[64,768]{1,0:T(8,128)(2,1)} %ti.1, bf16[64,768]{1,0:T(8,128)(2,1)} %tt.1, bf16[64,768]{1,0:T(8,128)(2,1)} %si.1, bf16[64,768]{1,0:T(8,128)(2,1)} %st.1, f32[2]{0:T(128)} %scales.1), custom_call_target="tpu_custom_call" | custom-call | tf_op jit(solution)/shard_map/pallas_call | solution.py:445
  48.3 0.7 %copy.7 = f32[1,64,768]{2,1,0:T(8,128)} copy(f32[1,64,768]{2,1,0:T(8,128)S(1)} %shard_map.55) | data formatting | bytes 393216

commit v7 on v6

--- a/solution.py
+++ b/solution.py
@@ -104,8 +104,10 @@
 
     barrier = pltpu.get_barrier_semaphore()
 
-    near = [sibling, up_y, down_y, device(xh, g, y2, z, core), across, beside]
-    near += [device(xh, g, y, mod(z + d, NZ), c) for d in (1, 7, 2, 6) for c in (0, 1)]
+    near = [device(xh, g, y, mod(z + d, NZ), c) for d in (2, 6) for c in (0, 1)]
+    near += [device(xh, g, y2, z, core)]
+    near += [device(xh, g, y, mod(z + d, NZ), c) for d in (1, 7) for c in (0, 1)]
+    near += [across, up_y, down_y, beside, sibling]
     for to in near:
         pl.semaphore_signal(barrier, inc=1, device_id=to, device_id_type=MESH)
 

time: 49.3 us -> 49.2 us (level)
  no operation moved by 1% of the time
where the time goes in v7:
time: 49.2 us; the launch traced here: 49 us
  Pallas kernels  48.3 us (98%)
  local copies, waits for them, and re-layouts  0.68 us (1%)
    pallas_call x1, Pallas kernels, per_device(): pl.pallas_call(kernel, out_shape=jax.ShapeDtypeStruct((1, N, width), F32)...  48.3 us

profile of v7, /device:TPU:2, one launch (start us, length us, event | category | flops | bytes accessed | tf_op | source)
XLA Modules:
  0.0 49.0 jit_solution(16517932137607093110)
XLA Ops:
  0.0 48.3 %shard_map.55 = f32[1,64,768]{2,1,0:T(8,128)S(1)} custom-call(bf16[64,768]{1,0:T(8,128)(2,1)} %ti.1, bf16[64,768]{1,0:T(8,128)(2,1)} %tt.1, bf16[64,768]{1,0:T(8,128)(2,1)} %si.1, bf16[64,768]{1,0:T(8,128)(2,1)} %st.1, f32[2]{0:T(128)} %scales.1), custom_call_target="tpu_custom_call" | custom-call | tf_op jit(solution)/shard_map/pallas_call | solution.py:447
  48.3 0.7 %copy.7 = f32[1,64,768]{2,1,0:T(8,128)} copy(f32[1,64,768]{2,1,0:T(8,128)S(1)} %shard_map.55) | data formatting | bytes 393216

commit v8 on v7

--- a/solution.py
+++ b/solution.py
@@ -16,6 +16,8 @@
 COLS = NY * 2 * N
 SENDS = 80
 FAR_FIRST = (8, 9, 7, 6, 10, 5, 11, 4, 12, 3, 13, 2, 14, 1, 15)
+FAR_FIRST_PLANE = (10, 9, 11, 6, 14, 2, 8, 5, 7, 13, 15, 1, 3, 4, 12)
+assert sorted(FAR_FIRST_PLANE) == sorted(FAR_FIRST)
 
 
 def mod(a, n):
@@ -264,20 +266,20 @@
         cstat[m, col_me] = jnp.concatenate(parts + rest, axis=0)
         rstat[m, row_me] = jnp.concatenate(row_lse + rest, axis=0)
 
-    def stat_copies(m, j):
+    def stat_copies(m, row_j, col_j):
         return [
             pltpu.make_async_remote_copy(
                 src_ref=ref.at[m, me], dst_ref=ref.at[m, me], send_sem=stsem.at[m, kind, j], recv_sem=sem.at[m, me],
                 device_id=peer(j)[1], device_id_type=MESH,
             )
-            for kind, (ref, sem, me, peer) in enumerate(
-                ((rstat, rssem, row_me, row_peer), (cstat, cssem, col_me, col_peer))
+            for kind, (ref, sem, me, peer, j) in enumerate(
+                ((rstat, rssem, row_me, row_peer, row_j), (cstat, cssem, col_me, col_peer, col_j))
             )
         ]
 
     def stats_start(m):
-        for j in FAR_FIRST:
-            for c in stat_copies(m, j):
+        for row_j, col_j in zip(FAR_FIRST, FAR_FIRST_PLANE):
+            for c in stat_copies(m, row_j, col_j):
                 c.start()
 
     def joined(all_):
@@ -329,7 +331,7 @@
 
         @pl.loop(1, 16)
         def _(j):
-            for c in stat_copies(m, j):
+            for c in stat_copies(m, j, j):
                 c.wait_send()
 
     factor = scale[1]

time: 49.2 us -> 49.2 us (level)
  no operation moved by 1% of the time
where the time goes in v8:
time: 49.2 us; the launch traced here: 49 us
  Pallas kernels  48.3 us (98%)
  local copies, waits for them, and re-layouts  0.68 us (1%)
    pallas_call x1, Pallas kernels, per_device(): pl.pallas_call(kernel, out_shape=jax.ShapeDtypeStruct((1, N, width), F32)...  48.3 us

profile of v8, /device:TPU:2, one launch (start us, length us, event | category | flops | bytes accessed | tf_op | source)
XLA Modules:
  0.0 49.0 jit_solution(11431531946802405602)
XLA Ops:
  0.0 48.3 %shard_map.55 = f32[1,64,768]{2,1,0:T(8,128)S(1)} custom-call(bf16[64,768]{1,0:T(8,128)(2,1)} %ti.1, bf16[64,768]{1,0:T(8,128)(2,1)} %tt.1, bf16[64,768]{1,0:T(8,128)(2,1)} %si.1, bf16[64,768]{1,0:T(8,128)(2,1)} %st.1, f32[2]{0:T(128)} %scales.1), custom_call_target="tpu_custom_call" | custom-call | tf_op jit(solution)/shard_map/pallas_call | solution.py:449
  48.3 0.7 %copy.7 = f32[1,64,768]{2,1,0:T(8,128)} copy(f32[1,64,768]{2,1,0:T(8,128)S(1)} %shard_map.55) | data formatting | bytes 393216
